TPU v7x, 128 devices: a whole 4x4x4 slice. The times are simulated.
128 devices in a mesh: dp: 32 (over z, x, core), tensor: 4 (over y).
Axes of the slice: x: 4, y: 4, z: 4, core: 2. Of those that a mesh axis runs over, the one named last changes fastest.
Arguments:
- activations: bfloat16 [4, 16384, 14336], P(None, 'dp', 'tensor'), may hold values from -6 to 6
- out_grads: bfloat16 [4, 16384, 4096], P(None, 'dp', 'tensor'), may hold values from -6 to 6
- proj_in: bfloat16 [4, 40, 14336], P(None, None, 'tensor'), may hold values from -0.046875 to 0.046875
- proj_out: bfloat16 [4, 40, 4096], P(None, None, 'tensor'), may hold values from -0.09375 to 0.09375
- lengths: int32 [128], P('dp'), may hold values from 16 to 128
- example_ids: int32 [128], P('dp'), may hold values from 0 to 127, each once
- prior_cov: bfloat16 [4, 1600, 1600], P('tensor'), as said below
- damping: float32 [4], P('tensor'), may hold values from 10 to 100
- queries: float32 [4, 64, 1600], P('tensor'), may hold values from -2 to 2
Outputs:
- scores: float32 [128, 64], P('dp')
Inputs may be any that keep to these rules, and one draw needn't show every extreme that they name: Each slot's tokens at positions from lengths on are padding. `example_ids`: a permutation of the examples over the slots. `prior_cov`: symmetric and positive definite.
All inputs are finite; a program needn't handle non-finite values.
Results may differ from a plain program's by a relative error of at most 0.0003.
Values sent between devices are 32-bit elements; how exact they have to be, the bound alone decides.
No kernel may reach another device: no remote copies, remote signals or barrier semaphores. Data moves between devices by JAX's collectives and lax.ppermute only.
A program may use at most 128 MiB of HBM per device.

v0:
```python
import jax
import jax.numpy as jnp
from jax import lax
from jax.sharding import PartitionSpec as P

KP = 40


def cut_along(x, dim, length):
    dims = x.shape
    pieces = x.reshape(*dims[:dim], length, dims[dim] // length, *dims[dim + 1 :])
    return jnp.moveaxis(pieces, dim, 0)


def sent_and_summed(x, axis, dim):
    length = lax.axis_size(axis)
    pieces = lax.all_to_all(cut_along(x, dim, length), axis, 0, 0, tiled=True)
    return jnp.sum(pieces, axis=0)


def side_by_side(arrays, axis, dim, along):
    ends, at = ([], 0)
    for a in arrays[:-1]:
        at += a.shape[along]
        ends.append(at)
    both = jnp.concatenate(arrays, axis=along)
    return tuple(jnp.split(sent_and_summed(both, axis, dim), ends, axis=along))


def per_device(
    activations, out_grads, proj_in, proj_out, lengths, example_ids, prior_cov, damping, queries
):
    ex_local = lengths.shape[0]
    seq_len = activations.shape[1] // ex_local
    proj_size = KP * KP
    live_mask = (jnp.arange(seq_len, dtype=jnp.int32)[None, :] < lengths[:, None]).astype(
        jnp.float32
    )
    in_parts = jnp.einsum("ltf,lkf->ltk", activations, proj_in, preferred_element_type=jnp.float32)
    out_parts = jnp.einsum("ltf,lkf->ltk", out_grads, proj_out, preferred_element_type=jnp.float32)
    in_owned, out_owned = side_by_side((in_parts, out_parts), "tensor", 0, 1)
    in_rows = in_owned[0]
    out_rows = out_owned[0]
    in_rows = in_rows.reshape(ex_local, seq_len, KP) * live_mask[:, :, None]
    out_rows = out_rows.reshape(ex_local, seq_len, KP)
    proj_grads = jnp.einsum(
        "est,esu->etu", out_rows, in_rows, precision=lax.Precision.HIGHEST
    ).reshape(ex_local, proj_size)
    piece_rows = lax.all_gather(proj_grads, "dp", axis=0, tiled=True)
    moment = jnp.dot(piece_rows.T, piece_rows, precision=lax.Precision.HIGHEST)
    examples_total = ex_local * lax.axis_size("dp")
    covariance = (
        prior_cov[0].astype(jnp.float32)
        + moment / examples_total
        + damping[0] * jnp.eye(proj_size, dtype=jnp.float32)
    )
    factor_lower = jnp.linalg.cholesky(covariance)
    forward_part = lax.linalg.triangular_solve(
        factor_lower, queries[0].T, left_side=True, lower=True
    )
    solved = lax.linalg.triangular_solve(
        factor_lower, forward_part, left_side=True, lower=True, transpose_a=True
    )
    layer_scores = jnp.dot(proj_grads, solved, precision=lax.Precision.HIGHEST)
    slot_scores = lax.psum(layer_scores, "tensor")
    one_hot = (example_ids[:, None] == jnp.arange(examples_total, dtype=jnp.int32)[None, :]).astype(
        jnp.float32
    )
    placed = jnp.einsum("se,sq->eq", one_hot, slot_scores, precision=lax.Precision.HIGHEST)
    return sent_and_summed(placed, "dp", 0)


def solution(mesh):
    in_specs = (
        P(None, "dp", "tensor"),
        P(None, "dp", "tensor"),
        P(None, None, "tensor"),
        P(None, None, "tensor"),
        P("dp"),
        P("dp"),
        P("tensor", None, None),
        P("tensor"),
        P("tensor", None, None),
    )
    out_specs = P("dp", None)
    return jax.shard_map(
        per_device, mesh=mesh, in_specs=in_specs, out_specs=out_specs, check_vma=False
    )
```

profile of v0, /device:TPU:0, one launch (start us, length us, event | category | flops | bytes accessed | tf_op | source)
XLA Modules:
  0.0 685.1 jit_solution(10697583175712387155)
XLA Ops:
  0.0 3.7 fusion.169
  3.7 9.5 %fusion.168 = f32[4,512,40]{1,2,0:T(8,128)S(1)} fusion(bf16[4,512,3584]{2,1,0:T(8,128)(2,1)} %param.9, bf16[4,40,3584]{2,1,0:T(8,128)(2,1)S(1)} %copy-done), kind=kOutput, calls=%fused_computation.430 | convolution fusion | flops 587202560 | bytes 16154624 | tf_op jit(solution)/shard_map/ltf,lkf->ltk/dot_general | solution.py:39
  14.1 4.6 all-to-all-start
  19.5 10.1 %all-to-all-done = f32[4,1,1024,40]{2,3,1,0:T(8,128)S(1)} async-done(((f32[4,1,1024,40]{2,3,1,0:T(8,128)}), f32[4,1,1024,40]{2,3,1,0:T(8,128)S(1)}, u32[]{:S(2)}, u32[]{:S(2)}) %all-to-all-start) | async-done | bytes 655392 | tf_op jit(solution)/shard_map/all_to_all | solution.py:17
  30.2 26.4 %all-gather = f32[32,4,1600]{2,1,0:T(4,128)S(1)} all-gather(f32[1,4,1600]{2,1,0:T(4,128)S(1)} %reshape.204), channel_id=1, replica_groups=mesh['dp'=32,'tensor'=4] {'dp'}, dimensions={0}, use_global_device_ids=true | all-gather | bytes 844800 | tf_op jit(solution)/shard_map/all_gather | solution.py:49
  56.9 16.0 %fusion = f32[1600,1600]{1,0:T(8,128)} fusion(f32[128,1600]{1,0:T(8,128)S(1)} %reshape.205, bf16[1,1600,1600]{2,1,0:T(8,128)(2,1)} %param.15, f32[]{:T(128)} %bitcast.243), kind=kOutput, calls=%fused_computation.4 | convolution fusion | flops 3947520000 | bytes 16179204 | tf_op jit(solution)/shard_map/dot_general | solution.py:50
  73.0 13.2 %copy.18 = f32[1600,1600]{0,1:T(8,128)} copy(f32[1600,1600]{1,0:T(8,128)} %fusion) | data formatting | bytes 20480000 | tf_op jit(solution)/shard_map/add | solution.py:53
  86.1 7.9 %fusion.1 = f32[1600,1600]{1,0:T(8,128)S(1)} fusion(f32[1600,1600]{1,0:T(8,128)} %fusion, f32[1600,1600]{0,1:T(8,128)} %copy.18), kind=kLoop, calls=%fused_computation.6 | loop fusion | flops 5120000 | bytes 30720000 | tf_op jit(solution)/shard_map/jit(cholesky)/div | solution.py:57
  94.1 4.0 copy-done.3
  98.1 11.7 %cholesky.371 = f32[128,128]{1,0:T(8,128)S(1)} custom-call(f32[128,128]{1,0:T(8,128)S(1)} %cholesky.973), custom_call_target="Cholesky" | custom-call | tf_op jit(solution)/shard_map/jit(cholesky)/cholesky | solution.py:57
  109.8 4.6 cholesky.401
  114.4 9.8 %custom-call.104 = f32[1,128,128]{1,2,0:T(8,128)S(1)} custom-call(f32[1,128,128]{2,1,0:T(8,128)S(1)} %get-tuple-element.59), custom_call_target="InvertDiagBlocksLowerTriangular" | custom-call | tf_op jit(solution)/shard_map/jit(cholesky)/cholesky | solution.py:57
  124.2 2.8 constant_dynamic-update-slice_fusion.160
  128.9 11.7 %cholesky.390 = f32[128,128]{1,0:T(8,128)S(1)} custom-call(f32[128,128]{1,0:T(8,128)S(1)} %cholesky.977), custom_call_target="Cholesky" | custom-call | tf_op jit(solution)/shard_map/jit(cholesky)/cholesky | solution.py:57
  141.3 10.2 %custom-call.105 = f32[1,128,128]{1,2,0:T(8,128)S(1)} custom-call(f32[1,128,128]{2,1,0:T(8,128)S(1)} %get-tuple-element.56), custom_call_target="InvertDiagBlocksLowerTriangular" | custom-call | tf_op jit(solution)/shard_map/jit(cholesky)/cholesky | solution.py:57
  153.0 2.8 convolution_subtract_fusion.2
  155.9 11.7 %cholesky.415 = f32[128,128]{1,0:T(8,128)S(1)} custom-call(f32[128,128]{1,0:T(8,128)S(1)} %cholesky.982), custom_call_target="Cholesky" | custom-call | tf_op jit(solution)/shard_map/jit(cholesky)/cholesky | solution.py:57
  168.2 9.8 %custom-call.106 = f32[1,128,128]{1,2,0:T(8,128)S(1)} custom-call(f32[1,128,128]{2,1,0:T(8,128)S(1)} %get-tuple-element.53), custom_call_target="InvertDiagBlocksLowerTriangular" | custom-call | tf_op jit(solution)/shard_map/jit(cholesky)/cholesky | solution.py:57
  179.6 3.6 convolution_subtract_fusion.1
  183.2 11.7 %cholesky.772 = f32[128,128]{1,0:T(8,128)S(1)} custom-call(f32[128,128]{1,0:T(8,128)S(1)} %cholesky.987), custom_call_target="Cholesky" | custom-call | tf_op jit(solution)/shard_map/jit(cholesky)/cholesky | solution.py:57
  195.6 9.8 %custom-call.107 = f32[1,128,128]{1,2,0:T(8,128)S(1)} custom-call(f32[1,128,128]{2,1,0:T(8,128)S(1)} %get-tuple-element.50), custom_call_target="InvertDiagBlocksLowerTriangular" | custom-call | tf_op jit(solution)/shard_map/jit(cholesky)/cholesky | solution.py:57
  206.9 3.7 convolution_subtract_fusion
  210.7 11.9 %cholesky.791 = f32[128,128]{1,0:T(8,128)S(1)} custom-call(f32[128,128]{1,0:T(8,128)S(1)} %cholesky.992), custom_call_target="Cholesky" | custom-call | tf_op jit(solution)/shard_map/jit(cholesky)/cholesky | solution.py:57
  223.2 9.8 %custom-call.108 = f32[1,128,128]{1,2,0:T(8,128)S(1)} custom-call(f32[1,128,128]{2,1,0:T(8,128)S(1)} %get-tuple-element.47), custom_call_target="InvertDiagBlocksLowerTriangular" | custom-call | tf_op jit(solution)/shard_map/jit(cholesky)/cholesky | solution.py:57
  234.5 4.0 fusion.17
  238.5 11.7 %cholesky.811 = f32[128,128]{1,0:T(8,128)S(1)} custom-call(f32[128,128]{1,0:T(8,128)S(1)} %cholesky.997), custom_call_target="Cholesky" | custom-call | tf_op jit(solution)/shard_map/jit(cholesky)/cholesky | solution.py:57
  250.8 9.8 %custom-call.109 = f32[1,128,128]{1,2,0:T(8,128)S(1)} custom-call(f32[1,128,128]{2,1,0:T(8,128)S(1)} %get-tuple-element.44), custom_call_target="InvertDiagBlocksLowerTriangular" | custom-call | tf_op jit(solution)/shard_map/jit(cholesky)/cholesky | solution.py:57
  262.3 4.0 fusion.20
  266.4 11.7 %cholesky.831 = f32[128,128]{1,0:T(8,128)S(1)} custom-call(f32[128,128]{1,0:T(8,128)S(1)} %cholesky.1002), custom_call_target="Cholesky" | custom-call | tf_op jit(solution)/shard_map/jit(cholesky)/cholesky | solution.py:57
  278.8 9.8 %custom-call.110 = f32[1,128,128]{1,2,0:T(8,128)S(1)} custom-call(f32[1,128,128]{2,1,0:T(8,128)S(1)} %get-tuple-element.41), custom_call_target="InvertDiagBlocksLowerTriangular" | custom-call | tf_op jit(solution)/shard_map/jit(cholesky)/cholesky | solution.py:57
  289.8 4.0 fusion.23
  293.9 11.9 %cholesky.851 = f32[128,128]{1,0:T(8,128)S(1)} custom-call(f32[128,128]{1,0:T(8,128)S(1)} %cholesky.1007), custom_call_target="Cholesky" | custom-call | tf_op jit(solution)/shard_map/jit(cholesky)/cholesky | solution.py:57
  306.4 9.8 %custom-call.111 = f32[1,128,128]{1,2,0:T(8,128)S(1)} custom-call(f32[1,128,128]{2,1,0:T(8,128)S(1)} %get-tuple-element.38), custom_call_target="InvertDiagBlocksLowerTriangular" | custom-call | tf_op jit(solution)/shard_map/jit(cholesky)/cholesky | solution.py:57
  317.4 3.8 fusion.26
  321.2 11.7 %cholesky.871 = f32[128,128]{1,0:T(8,128)S(1)} custom-call(f32[128,128]{1,0:T(8,128)S(1)} %cholesky.1012), custom_call_target="Cholesky" | custom-call | tf_op jit(solution)/shard_map/jit(cholesky)/cholesky | solution.py:57
  333.6 10.2 %custom-call.112 = f32[1,128,128]{1,2,0:T(8,128)S(1)} custom-call(f32[1,128,128]{2,1,0:T(8,128)S(1)} %get-tuple-element.35), custom_call_target="InvertDiagBlocksLowerTriangular" | custom-call | tf_op jit(solution)/shard_map/jit(cholesky)/cholesky | solution.py:57
  344.8 3.6 fusion.29
  348.5 11.7 %cholesky.891 = f32[128,128]{1,0:T(8,128)S(1)} custom-call(f32[128,128]{1,0:T(8,128)S(1)} %cholesky.1017), custom_call_target="Cholesky" | custom-call | tf_op jit(solution)/shard_map/jit(cholesky)/cholesky | solution.py:57
  360.8 9.8 %custom-call.113 = f32[1,128,128]{1,2,0:T(8,128)S(1)} custom-call(f32[1,128,128]{2,1,0:T(8,128)S(1)} %get-tuple-element.32), custom_call_target="InvertDiagBlocksLowerTriangular" | custom-call | tf_op jit(solution)/shard_map/jit(cholesky)/cholesky | solution.py:57
  371.6 3.1 fusion.32
  374.7 11.9 %cholesky.911 = f32[128,128]{1,0:T(8,128)S(1)} custom-call(f32[128,128]{1,0:T(8,128)S(1)} %cholesky.1022), custom_call_target="Cholesky" | custom-call | tf_op jit(solution)/shard_map/jit(cholesky)/cholesky | solution.py:57
  387.2 9.8 %custom-call.114 = f32[1,128,128]{1,2,0:T(8,128)S(1)} custom-call(f32[1,128,128]{2,1,0:T(8,128)S(1)} %get-tuple-element.29), custom_call_target="InvertDiagBlocksLowerTriangular" | custom-call | tf_op jit(solution)/shard_map/jit(cholesky)/cholesky | solution.py:57
  397.9 2.5 convolution_subtract_fusion.4
  400.5 11.7 %cholesky.931 = f32[128,128]{1,0:T(8,128)S(1)} custom-call(f32[128,128]{1,0:T(8,128)S(1)} %cholesky.1027), custom_call_target="Cholesky" | custom-call | tf_op jit(solution)/shard_map/jit(cholesky)/cholesky | solution.py:57
  412.9 9.8 %custom-call.115 = f32[1,128,128]{1,2,0:T(8,128)S(1)} custom-call(f32[1,128,128]{2,1,0:T(8,128)S(1)} %get-tuple-element.26), custom_call_target="InvertDiagBlocksLowerTriangular" | custom-call | tf_op jit(solution)/shard_map/jit(cholesky)/cholesky | solution.py:57
  425.1 5.8 cholesky.952
  447.7 4.8 select_select_fusion
  452.6 4.0 copy-done.2
  456.5 34.0 %while.1 = (s32[]{:T(128)}, f32[1600,1600]{1,0:T(8,128)}, s32[12,2]{0,1:T(2,128)S(1)}, f32[12,128,128]{2,1,0:T(8,128)S(1)}, s32[]{:T(128)}) while((s32[]{:T(128)}, f32[1600,1600]{1,0:T(8,128)}, s32[12,2]{0,1:T(2,128)S(1)}, f32[12,128,128]{2,1,0:T(8,128)S(1)}, s32[]{:T(128)}) %tuple.125), condition=%wide.while_cond, body=%wide.while_body.sunk | while | flops 2 | bytes 131189 | solution.py:61
  457.1 2.2 bitcast_dynamic-update-slice_fusion.2
  460.0 2.2 bitcast_dynamic-update-slice_fusion.2
  462.8 2.2 bitcast_dynamic-update-slice_fusion.2
  465.6 2.2 bitcast_dynamic-update-slice_fusion.2
  468.5 2.2 bitcast_dynamic-update-slice_fusion.2
  471.3 2.2 bitcast_dynamic-update-slice_fusion.2
  474.1 2.2 bitcast_dynamic-update-slice_fusion.2
  477.0 2.2 bitcast_dynamic-update-slice_fusion.2
  479.8 2.2 bitcast_dynamic-update-slice_fusion.2
  482.6 2.2 bitcast_dynamic-update-slice_fusion.2
  485.4 2.2 bitcast_dynamic-update-slice_fusion.2
  488.3 2.2 bitcast_dynamic-update-slice_fusion.2
  490.7 127.9 %custom-call.116 = f32[13,128,128]{1,2,0:T(8,128)S(1)} custom-call(f32[13,128,128]{2,1,0:T(8,128)S(1)} %pad_maximum_fusion), custom_call_target="InvertDiagBlocksLowerTriangular" | custom-call | tf_op jit(solution)/shard_map/triangular_solve | solution.py:61
  661.2 8.9 %psum.7 = f32[4,64]{1,0:T(4,128)S(1)} all-reduce(f32[4,64]{1,0:T(4,128)S(1)} %fusion.170), channel_id=1, replica_groups=mesh['dp'=32,'tensor'=4] {'tensor'}, use_global_device_ids=true, to_apply=%region_27.28 | all-reduce | flops 256 | bytes 2048 | tf_op jit(solution)/shard_map/psum | solution.py:65
  670.5 12.4 %all_to_all.10 = f32[32,1,256]{2,1,0:T(1,128)S(1)} all-to-all(f32[32,1,256]{2,1,0:T(1,128)S(1)} %reshape.207), channel_id=1, replica_groups=mesh['dp'=32,'tensor'=4] {'dp'}, dimensions={0} | all-to-all | bytes 65536 | tf_op jit(solution)/shard_map/all_to_all | solution.py:17
  (235 shorter events, 86.4 us)
Async XLA Ops:
  0.0 3.7 copy-start
  0.0 19.4 %copy-start.6 = (s32[4]{0:T(128)S(1)}, s32[4]{0:T(128)}, u32[]{:S(2)}) copy-start(s32[4]{0:T(128)} %param.13) | copy-start | bytes 52
  14.1 15.5 %all-to-all-start = ((f32[4,1,1024,40]{2,3,1,0:T(8,128)}), f32[4,1,1024,40]{2,3,1,0:T(8,128)S(1)}, u32[]{:S(2)}, u32[]{:S(2)}) async-start(f32[4,1,1024,40]{2,3,1,0:T(8,128)} %maximum_bitcast_fusion), calls=%async_computation | async-start | bytes 1310720 | tf_op jit(solution)/shard_map/all_to_all | solution.py:17
  94.1 4.0 copy-start.3
  447.7 170.9 %copy-start.4 = (f32[1,64,1600]{2,1,0:T(8,128)S(1)}, f32[1,64,1600]{2,1,0:T(8,128)}, u32[]{:S(2)}) copy-start(f32[1,64,1600]{2,1,0:T(8,128)} %param.17) | copy-start | bytes 1228804
  452.5 4.0 copy-start.2
  629.6 40.4 %copy-start.5 = (s32[4]{0:T(128)S(1)}, s32[4]{0:T(128)}, u32[]{:S(2)}) copy-start(s32[4]{0:T(128)} %param.14) | copy-start | bytes 52
  629.8 55.0 %copy-start.1 = (bf16[4,40,3584]{2,1,0:T(8,128)(2,1)S(1)}, bf16[4,40,3584]{2,1,0:T(8,128)(2,1)}, u32[]{:S(2)}) copy-start(bf16[4,40,3584]{2,1,0:T(8,128)(2,1)} %param.11) | copy-start | bytes 3440644
where the time goes:
time: 691 us; the launch traced here: 685 us
  other arithmetic  424 us (61%)
  matrix products  127 us (18%)
  local copies, waits for them, and re-layouts  61.2 us (9%)
  blocking collectives  47.7 us (7%)
  between operations  10.4 us (2%)
  waiting for transfers between devices  10.1 us (1%)
    another operation x50, other arithmetic, per_device(): factor_lower = jnp.linalg.cholesky(covariance)  281 us
    another operation x7, other arithmetic, per_device(): lax.linalg.triangular_solve(factor_lower, forward_part, left_side=True, l...  133 us
    another operation x24, matrix products, per_device(): factor_lower = jnp.linalg.cholesky(covariance)  55.4 us
    another operation x36, local copies, waits for them, and re-layouts  33.7 us
    all_gather x1, blocking collectives, per_device(): piece_rows = lax.all_gather(proj_grads, 'dp', axis=0, tiled=True)  26.4 us
    another operation x25, matrix products, per_device(): lax.linalg.triangular_solve(factor_lower, queries[0].T, left_side=True, l...  21.1 us
    another operation x25, matrix products, per_device(): lax.linalg.triangular_solve(factor_lower, forward_part, left_side=True, l...  19.7 us
    dot_general x1, matrix products, per_device(): moment = jnp.dot(piece_rows.T, piece_rows, precision=lax.Precision.HIGHEST)  16 us
  transfers between devices with their start and end apart: 1, of which 1 were waited for; matrix products, arithmetic and copies ran while one was open for 0% of the time, Pallas kernels for 0%

commit v1 on v0

v1 whole, which is shorter than its diff:
```python
import jax
import jax.numpy as jnp
from jax import lax
from jax.experimental import pallas as pl
from jax.experimental.pallas import tpu as pltpu
from jax.sharding import PartitionSpec as P

KP = 40
B = 128


def split(x):
    high = x.astype(jnp.bfloat16)
    low = (x - high.astype(jnp.float32)).astype(jnp.bfloat16)
    return high, low


def down(row):
    return jnp.broadcast_to(row, (8, B))


def block_inverse(rows):
    lane = lax.broadcasted_iota(jnp.int32, (8, B), 1)
    sub = lax.broadcasted_iota(jnp.int32, (8, B), 0)
    rows = list(rows)
    for g in range(16):
        first = 8 * g
        columns = [
            [jnp.broadcast_to(rows[h][:, first + m : first + m + 1], (8, B)) for m in range(8)]
            for h in range(16)
        ]
        pivots = columns[g]
        in_pivot = (lane >= first) & (lane < first + 8)
        panel = jnp.where(in_pivot, jnp.where(lane - first == sub, 1.0, 0.0), rows[g])
        for j in range(8):
            r = down((1.0 / pivots[j])[j : j + 1])
            others = jnp.where(sub == j, 0.0, pivots[j])
            scaled = down(panel[j : j + 1]) * r
            panel = jnp.where(sub == j, scaled, panel) - others * scaled
            for m in range(j + 1, 8):
                scaled = down(pivots[m][j : j + 1]) * r
                pivots[m] = jnp.where(sub == j, scaled, pivots[m]) - others * scaled
        spread = [down(panel[m : m + 1]) for m in range(8)]
        for h in [(g + 1 + t) % 16 for t in range(15)]:
            total = columns[h][0] * spread[0]
            for m in range(1, 8):
                total = total + columns[h][m] * spread[m]
            rows[h] = jnp.where(in_pivot, 0.0, rows[h]) - total
        rows[g] = panel
    return rows


def solve_kernel(prior_ref, damp_ref, grads_ref, right_ref, out_ref, work, terms, inverse):
    size = prior_ref.shape[0]
    blocks = pl.cdiv(size, B)
    width = (blocks + 1) * B
    tail = blocks * B
    examples = grads_ref.shape[0]
    work[...] = jnp.zeros((width, width), jnp.float32)
    work[0:size, 0:size] = prior_ref[...].astype(jnp.float32)
    work[tail:width, 0:size] = right_ref[...]
    work[0:size, tail:width] = right_ref[...].T
    r = lax.broadcasted_iota(jnp.int32, (B, B), 0)
    c = lax.broadcasted_iota(jnp.int32, (B, B), 1)
    for k in range(blocks):
        here = slice(k * B, (k + 1) * B)
        work[here, here] += jnp.where(r == c, jnp.where(r + k * B < size, damp_ref[0], 1.0), 0.0)

    def set_terms(x, at):
        high, low = split(x)
        to = at + x.shape[1]
        terms[0:B, at:to] = high
        terms[B : 2 * B, at:to] = low
        terms[2 * B : 3 * B, at:to] = high

    def product(left, at):
        high, low = split(left)
        left = jnp.concatenate([high, high, low], axis=1)
        return jnp.dot(left, terms[:, at:], preferred_element_type=jnp.float32)

    terms[...] = jnp.zeros_like(terms)
    set_terms(grads_ref[...] * (1.0 / examples), 0)
    grads_t = grads_ref[...].T
    for k in range(blocks):
        here = slice(k * B, min((k + 1) * B, size))
        work[here, :] += product(grads_t[here], 0)

    def eliminate(k, at):
        first = pl.multiple_of(k * B, B)
        block = work[pl.ds(first, B), pl.ds(first, B)]
        for h, piece in enumerate(block_inverse([block[8 * h : 8 * h + 8] for h in range(16)])):
            inverse[8 * h : 8 * h + 8] = piece
        panel = jnp.dot(
            inverse[...],
            work[pl.ds(first, B), at:],
            preferred_element_type=jnp.float32,
            precision=lax.Precision.HIGHEST,
        )
        set_terms(panel, at)

        def update(i, carry):
            rows = pl.ds(pl.multiple_of(i * B, B), B)
            work[rows, at:] -= product(work[rows, pl.ds(first, B)], at)
            return carry

        lax.fori_loop(k + 1, blocks + 1, update, 0)

    starts = (0, 4, 8)
    for start, stop in zip(starts, (*starts[1:], blocks)):

        def body(k, carry, at=start * B):
            eliminate(k, at)
            return carry

        lax.fori_loop(start, stop, body, 0)
    out_ref[...] = -work[tail:width, tail:width]


def scores_of(prior, damping, grads, right):
    width = (pl.cdiv(prior.shape[0], B) + 1) * B
    vmem = pl.BlockSpec(memory_space=pltpu.VMEM)
    return pl.pallas_call(
        solve_kernel,
        out_shape=jax.ShapeDtypeStruct((B, B), jnp.float32),
        in_specs=[vmem, pl.BlockSpec(memory_space=pltpu.SMEM), vmem, vmem],
        out_specs=vmem,
        scratch_shapes=[
            pltpu.VMEM((width, width), jnp.float32),
            pltpu.VMEM((3 * B, width), jnp.bfloat16),
            pltpu.VMEM((B, B), jnp.float32),
        ],
        compiler_params=pltpu.CompilerParams(vmem_limit_bytes=60 * 2**20),
    )(prior, damping, grads, right)


def cut_along(x, dim, length):
    dims = x.shape
    pieces = x.reshape(*dims[:dim], length, dims[dim] // length, *dims[dim + 1 :])
    return jnp.moveaxis(pieces, dim, 0)


def sent_and_summed(x, axis, dim):
    length = lax.axis_size(axis)
    pieces = lax.all_to_all(cut_along(x, dim, length), axis, 0, 0, tiled=True)
    return jnp.sum(pieces, axis=0)


def per_device(
    activations, out_grads, proj_in, proj_out, lengths, example_ids, prior_cov, damping, queries
):
    ex_local = lengths.shape[0]
    seq_len = activations.shape[1] // ex_local
    tokens = activations.shape[1]
    proj_size = KP * KP
    n_query = queries.shape[1]
    live_mask = (jnp.arange(seq_len, dtype=jnp.int32)[None, :] < lengths[:, None]).astype(
        jnp.float32
    )
    in_parts = jnp.einsum("ltf,lkf->ltk", activations, proj_in, preferred_element_type=jnp.float32)
    out_parts = jnp.einsum("ltf,lkf->ltk", out_grads, proj_out, preferred_element_type=jnp.float32)
    owned = sent_and_summed(jnp.concatenate([in_parts, out_parts], axis=1), "tensor", 0)[0]
    in_rows = owned[:tokens].reshape(ex_local, seq_len, KP) * live_mask[:, :, None]
    out_rows = owned[tokens:].reshape(ex_local, seq_len, KP)
    proj_grads = jnp.einsum(
        "est,esu->etu", out_rows, in_rows, precision=lax.Precision.HIGHEST
    ).reshape(ex_local, proj_size)
    sent = jnp.concatenate([proj_grads, example_ids.astype(jnp.float32)[:, None]], axis=1)
    gathered = lax.all_gather(sent, "dp", axis=0, tiled=True)
    grads = gathered[:, :proj_size]
    ids = gathered[:, proj_size].astype(jnp.int32)
    mine = lax.axis_index("dp") * ex_local + jnp.arange(ex_local, dtype=jnp.int32)
    pick = (ids[None, :] == mine[:, None]).astype(jnp.float32)
    picked = jnp.dot(pick, grads, precision=lax.Precision.HIGHEST)
    right = jnp.concatenate(
        [queries[0], picked, jnp.zeros((B - n_query - ex_local, proj_size), jnp.float32)], axis=0
    )
    product = scores_of(prior_cov[0], damping, grads, right)
    layer_scores = product[n_query : n_query + ex_local, :n_query]
    return lax.psum(layer_scores, "tensor")


def solution(mesh):
    in_specs = (
        P(None, "dp", "tensor"),
        P(None, "dp", "tensor"),
        P(None, None, "tensor"),
        P(None, None, "tensor"),
        P("dp"),
        P("dp"),
        P("tensor", None, None),
        P("tensor"),
        P("tensor", None, None),
    )
    out_specs = P("dp", None)
    return jax.shard_map(
        per_device, mesh=mesh, in_specs=in_specs, out_specs=out_specs, check_vma=False
    )
```

time: 691 us -> 196 us (0.28)
  other arithmetic: 424 us -> 2.33 us
  Pallas kernels: 0 us -> 126 us
  matrix products: 127 us -> 13.7 us
  local copies, waits for them, and re-layouts: 61.2 us -> 2.61 us
  blocking collectives: 47.7 us -> 35.7 us
  between operations: 10.4 us -> 0.79 us
    another operation x57 -> x0, other arithmetic: 414 us -> none  [the longest x50 281 us: per_device(): factor_lower = jnp.linalg.cholesky(covariance)]
    pallas_call x0 -> x1, Pallas kernels: none -> 126 us  [scores_of(): pl.pallas_call(solve_kernel, out_shape=jax.ShapeDtypeStruct((B, B), jnp.f...]
    another operation x74 -> x0, matrix products: 96.3 us -> none  [the longest x24 55.4 us: per_device(): factor_lower = jnp.linalg.cholesky(covariance)]
    another operation x62 -> x0, local copies, waits for them, and re-layouts: 38.5 us -> none
    dot_general x3 -> x1, matrix products: 16.8 us -> 0.41 us  [per_device(): picked = jnp.dot(pick, grads, precision=lax.Precision.HIGHEST)]
    add x1 -> x0, local copies, waits for them, and re-layouts: 13.2 us -> none  [per_device(): prior_cov[0].astype(jnp.float32) + moment / examples_total]
    all_to_all x1 -> x0, blocking collectives: 12.4 us -> none  [sent_and_summed(): pieces = lax.all_to_all(cut_along(x, dim, length), axis, 0, 0, tiled=True)]
    div x1 -> x0, other arithmetic: 7.94 us -> none  [per_device(): factor_lower = jnp.linalg.cholesky(covariance)]
where the time goes in v1:
time: 196 us
  Pallas kernels  126 us (64%)
  blocking collectives  35.7 us (18%)
  matrix products  13.7 us (7%)
  waiting for transfers between devices  9.96 us (5%)
  starting transfers between devices  4.57 us (2%)
  local copies, waits for them, and re-layouts  2.61 us (1%)
  other arithmetic  2.33 us (1%)
    pallas_call x1, Pallas kernels, scores_of(): pl.pallas_call(solve_kernel, out_shape=jax.ShapeDtypeStruct((B, B), jnp.f...  126 us
    all_gather x1, blocking collectives, per_device(): gathered = lax.all_gather(sent, 'dp', axis=0, tiled=True)  26.2 us
    all_to_all x1, waiting for transfers between devices, sent_and_summed(): pieces = lax.all_to_all(cut_along(x, dim, length), axis, 0, 0, tiled=True)  9.96 us
    dot_general x1, matrix products, per_device(): jnp.einsum('ltf,lkf->ltk', activations, proj_in, preferred_element_type=j...  9.51 us
    psum x1, blocking collectives, per_device(): return lax.psum(layer_scores, 'tensor')  9.44 us
    all_to_all x1, starting transfers between devices, sent_and_summed(): pieces = lax.all_to_all(cut_along(x, dim, length), axis, 0, 0, tiled=True)  4.57 us
  transfers between devices with their start and end apart: 1, of which 1 were waited for; matrix products, arithmetic and copies ran while one was open for 0% of the time, Pallas kernels for 0%

profile of v1, /device:TPU:0, one launch (start us, length us, event | category | flops | bytes accessed | tf_op | source)
XLA Modules:
  0.0 195.9 jit_solution(2337830593042404131)
XLA Ops:
  0.0 0.0 copy-start
  0.0 0.0 copy-start.3
  0.0 1.3 copy-done
  1.3 9.5 %fusion.11 = f32[4,512,40]{1,2,0:T(8,128)S(1)} fusion(bf16[4,512,3584]{2,1,0:T(8,128)(2,1)} %param.9, bf16[4,40,3584]{2,1,0:T(8,128)(2,1)S(1)} %copy-done), kind=kOutput, calls=%fused_computation.19 | convolution fusion | flops 587202560 | bytes 16154624 | tf_op jit(solution)/shard_map/ltf,lkf->ltk/dot_general | solution.py:159
  10.8 0.0 copy-done.3
  10.8 0.0 copy-start.5
  10.8 0.0 copy-start.4
  10.8 3.6 %fusion.12 = f32[4,512,40]{1,2,0:T(8,128)S(1)} fusion(bf16[4,512,1024]{2,1,0:T(8,128)(2,1)} %param.10, bf16[4,40,1024]{2,1,0:T(8,128)(2,1)S(1)} %copy-done.3), kind=kOutput, calls=%fused_computation.20 | convolution fusion | flops 167772160 | bytes 4849664 | tf_op jit(solution)/shard_map/ltf,lkf->ltk/dot_general | solution.py:160
  14.4 0.0 copy-start.2
  14.4 0.9 maximum_bitcast_fusion
  15.3 4.6 %all-to-all-start = ((f32[4,1,1024,40]{2,3,1,0:T(8,128)}), f32[4,1,1024,40]{2,3,1,0:T(8,128)S(1)}, u32[]{:S(2)}, u32[]{:S(2)}) async-start(f32[4,1,1024,40]{2,3,1,0:T(8,128)} %maximum_bitcast_fusion), calls=%async_computation | async-start | bytes 1310720 | tf_op jit(solution)/shard_map/all_to_all | solution.py:144
  20.5 0.0 copy-done.5
  20.5 0.1 copy.17
  20.6 0.1 pad.2.clone
  20.7 0.0 copy-done.4
  20.7 0.1 fusion.4
  20.8 10.0 %all-to-all-done = f32[4,1,1024,40]{2,3,1,0:T(8,128)S(1)} async-done(((f32[4,1,1024,40]{2,3,1,0:T(8,128)}), f32[4,1,1024,40]{2,3,1,0:T(8,128)S(1)}, u32[]{:S(2)}, u32[]{:S(2)}) %all-to-all-start) | async-done | bytes 655392 | tf_op jit(solution)/shard_map/all_to_all | solution.py:144
  30.9 0.3 fusion
  31.2 0.1 reshape.52
  31.3 0.1 maximum_bitcast_fusion.1
  31.4 26.2 %all-gather = f32[32,4,1601]{2,1,0:T(4,128)S(1)} all-gather(f32[1,4,1601]{2,1,0:T(4,128)S(1)} %maximum_bitcast_fusion.1), channel_id=1, replica_groups=mesh['dp'=32,'tensor'=4] {'dp'}, dimensions={0}, use_global_device_ids=true | all-gather | bytes 845328 | tf_op jit(solution)/shard_map/all_gather | solution.py:168
  57.6 0.3 reshape.54
  57.9 0.0 copy-start.1
  57.9 0.2 fusion.3
  58.1 0.4 fusion.5
  58.5 0.0 copy-done.2
  58.5 1.1 maximum_maximum_fusion.right_ref
  59.5 0.0 copy-done.1
  59.5 126.3 %shard_map.91 = f32[128,128]{1,0:T(8,128)} custom-call(bf16[1600,1600]{1,0:T(8,128)(2,1)} %bitcast.24, f32[1]{0:T(128)S(6)} %copy.22.damp_ref, f32[128,1600]{1,0:T(8,128)} %bitcast.23, f32[128,1600]{1,0:T(8,128)} %maximum_maximum_fusion.right_ref), custom_call_target="tpu_custom_call" | custom-call | tf_op jit(solution)/shard_map/pallas_call | solution.py:122
  185.8 0.7 slice.26
  186.5 9.4 %psum.7 = f32[4,64]{1,0:T(4,128)} all-reduce(f32[4,64]{1,0:T(4,128)S(1)} %slice.26), channel_id=1, replica_groups=mesh['dp'=32,'tensor'=4] {'tensor'}, use_global_device_ids=true, to_apply=%region_1.0 | all-reduce | flops 256 | bytes 2048 | tf_op jit(solution)/shard_map/psum | solution.py:179
  (9 shorter events, 0.1 us)
Async XLA Ops:
  0.0 1.3 copy-start
  0.0 10.8 %copy-start.3 = (bf16[4,40,1024]{2,1,0:T(8,128)(2,1)S(1)}, bf16[4,40,1024]{2,1,0:T(8,128)(2,1)}, u32[]{:S(2)}) copy-start(bf16[4,40,1024]{2,1,0:T(8,128)(2,1)} %param.12) | copy-start | bytes 983044
  10.8 9.7 %copy-start.5 = (s32[4]{0:T(128)S(1)}, s32[4]{0:T(128)}, u32[]{:S(2)}) copy-start(s32[4]{0:T(128)} %param.14) | copy-start | bytes 52
  10.8 9.9 %copy-start.4 = (s32[4]{0:T(128)S(1)}, s32[4]{0:T(128)}, u32[]{:S(2)}) copy-start(s32[4]{0:T(128)} %param.13) | copy-start | bytes 52
  14.4 44.1 %copy-start.2 = (f32[1,64,1600]{2,1,0:T(8,128)S(1)}, f32[1,64,1600]{2,1,0:T(8,128)}, u32[]{:S(2)}) copy-start(f32[1,64,1600]{2,1,0:T(8,128)} %param.17) | copy-start | bytes 1228804
  15.3 15.5 %all-to-all-start = ((f32[4,1,1024,40]{2,3,1,0:T(8,128)}), f32[4,1,1024,40]{2,3,1,0:T(8,128)S(1)}, u32[]{:S(2)}, u32[]{:S(2)}) async-start(f32[4,1,1024,40]{2,3,1,0:T(8,128)} %maximum_bitcast_fusion), calls=%async_computation | async-start | bytes 1310720 | tf_op jit(solution)/shard_map/all_to_all | solution.py:144
  57.9 1.7 copy-start.1

commit v2 on v1

v2 whole, which is shorter than its diff:
```python
import jax
import jax.numpy as jnp
from jax import lax
from jax.experimental import pallas as pl
from jax.experimental.pallas import tpu as pltpu
from jax.sharding import PartitionSpec as P

KP = 40
B = 128
S = 16
STARTS = (0, 3, 6, 9)


def split(x):
    high = x.astype(jnp.bfloat16)
    low = (x - high.astype(jnp.float32)).astype(jnp.bfloat16)
    return high, low


def down(row):
    return jnp.broadcast_to(row, (8, B))


def block_inverse(block):
    lane = lax.broadcasted_iota(jnp.int32, (8, B), 1)
    sub = lax.broadcasted_iota(jnp.int32, (8, B), 0)
    rows = [block[8 * h : 8 * h + 8] for h in range(16)]

    def columns(piece, first):
        return [jnp.broadcast_to(piece[:, first + m : first + m + 1], (8, B)) for m in range(S)]

    for g in range(B // S):
        first = S * g
        here = (2 * g, 2 * g + 1)
        in_pivot = (lane >= first) & (lane < first + S)
        cols = [list(pair) for pair in zip(*(columns(rows[h], first) for h in here))]
        after = (2 * g + 2, 2 * g + 3) if g + 1 < B // S else ()
        next_cols = [columns(rows[h], first) for h in after]
        panel = [
            jnp.where(in_pivot, jnp.where(lane - first == sub + 8 * q, 1.0, 0.0), rows[h])
            for q, h in enumerate(here)
        ]
        for j in range(S):
            a, s = j // 8, j % 8
            pivot = cols[j]
            r = down((1.0 / pivot[a])[s : s + 1])
            others = jnp.where(sub == s, 0.0, pivot[a])
            for item in (*cols[j + 1 :], panel):
                scaled = down(item[a][s : s + 1]) * r
                item[a] = jnp.where(sub == s, scaled, item[a]) - others * scaled
                item[1 - a] = item[1 - a] - pivot[1 - a] * scaled
        high, low = split(jnp.concatenate(panel, axis=0))
        both = jnp.concatenate([high, low], axis=1)
        parts = [jnp.zeros((S, 2 * B), jnp.bfloat16)] * (B // S)
        parts[g] = both
        right = jnp.concatenate(parts + parts, axis=0)
        left = jnp.concatenate(split(jnp.concatenate(rows, axis=0)), axis=1)
        change = jnp.dot(left, right, preferred_element_type=jnp.float32)
        change = change[:, :B] + change[:, B:]
        fresh = []
        for h in range(16):
            if h in here:
                fresh.append(panel[h - here[0]])
                continue
            kept = jnp.where(in_pivot, 0.0, rows[h])
            if h in after:
                terms = [
                    c * down(panel[m // 8][m % 8 : m % 8 + 1])
                    for m, c in enumerate(next_cols[h - after[0]])
                ]
                while len(terms) > 1:
                    terms = [x + y for x, y in zip(terms[::2], terms[1::2])]
                fresh.append(kept - terms[0])
            else:
                fresh.append(kept - change[8 * h : 8 * h + 8])
        rows = fresh
    return jnp.concatenate(rows, axis=0)


def solve_kernel(prior_ref, damp_ref, grads_ref, right_ref, out_ref, work, left, terms):
    size = prior_ref.shape[0]
    blocks = pl.cdiv(size, B)
    tail = blocks * B
    examples = grads_ref.shape[0]
    whole = size // B * B
    r = lax.broadcasted_iota(jnp.int32, (B, B), 0)
    c = lax.broadcasted_iota(jnp.int32, (B, B), 1)

    def set_left(rows, x):
        high, low = split(x)
        left[rows, 0:B] = high
        left[rows, B : 2 * B] = high
        left[rows, 2 * B :] = low

    def set_terms(rows, x):
        high, low = split(x)
        terms[rows, 0:B] = high
        terms[rows, B : 2 * B] = low
        terms[rows, 2 * B :] = high

    for k in range(blocks):
        here = slice(k * B, min((k + 1) * B, size))
        work[here, 0 : here.stop] = prior_ref[here, 0 : here.stop].astype(jnp.float32)
        if here.stop < (k + 1) * B:
            work[here.stop : (k + 1) * B, 0 : (k + 1) * B] = jnp.zeros(((k + 1) * B - size, (k + 1) * B), jnp.float32)
            work[here, here.stop : (k + 1) * B] = jnp.zeros((size - k * B, (k + 1) * B - size), jnp.float32)
        spot = slice(k * B, (k + 1) * B)
        work[spot, spot] += jnp.where(r == c, jnp.where(r + k * B < size, damp_ref[0], 1.0), 0.0)
    work[tail : tail + B, 0:size] = right_ref[...]
    work[tail : tail + B, size:tail] = jnp.zeros((B, tail - size), jnp.float32)
    work[tail : tail + B, tail : tail + B] = jnp.zeros((B, B), jnp.float32)
    left[...] = jnp.zeros_like(left)
    terms[...] = jnp.zeros_like(terms)
    grads_t = grads_ref[...].T
    set_left(slice(0, size), grads_t)
    set_terms(slice(0, size), grads_t * (-1.0 / examples))

    def product(x, y):
        return lax.dot_general(x, y, (((1,), (1,)), ((), ())), preferred_element_type=jnp.float32)

    def step(k, count):
        def at(t, n=1):
            return pl.ds(pl.multiple_of((k + t) * B, B), n * B)

        inverse = block_inverse(work[at(0), at(0)] - product(left[at(0), :], terms[at(0), :]))
        for t in range(0, count, 2):
            n = min(2, count - t)
            rows = at(t, count - t)
            work[rows, at(t, n)] -= product(left[rows, :], terms[at(t, n), :])
        rows = at(1, count - 1)
        set_left(rows, work[rows, at(0)])
        high, low = split(inverse)
        stacked = jnp.concatenate([high, low, high], axis=0)
        set_terms(rows, jnp.dot(left[rows, :], stacked, preferred_element_type=jnp.float32))

    for start, stop in zip(STARTS, (*STARTS[1:], blocks)):

        def body(k, carry, count=blocks + 1 - start):
            step(k, count)
            return carry

        lax.fori_loop(start, stop, body, 0)
    last = slice(tail, tail + B)
    out_ref[...] = product(left[last, :], terms[last, :]) - work[last, last]


def scores_of(prior, damping, grads, right):
    blocks = pl.cdiv(prior.shape[0], B)
    most = max(b - a for a, b in zip(STARTS, (*STARTS[1:], blocks)))
    width = (blocks + most) * B
    vmem = pl.BlockSpec(memory_space=pltpu.VMEM)
    return pl.pallas_call(
        solve_kernel,
        out_shape=jax.ShapeDtypeStruct((B, B), jnp.float32),
        in_specs=[vmem, pl.BlockSpec(memory_space=pltpu.SMEM), vmem, vmem],
        out_specs=vmem,
        scratch_shapes=[
            pltpu.VMEM((width, width), jnp.float32),
            pltpu.VMEM((width, 3 * B), jnp.bfloat16),
            pltpu.VMEM((width, 3 * B), jnp.bfloat16),
        ],
        compiler_params=pltpu.CompilerParams(vmem_limit_bytes=60 * 2**20),
    )(prior, damping, grads, right)


def to_layer(parts, axis):
    length = lax.axis_size(axis)
    me = lax.axis_index(axis)
    total = lax.dynamic_index_in_dim(parts, me, 0, keepdims=False)
    for d in (1, length - 1, *range(2, length - 1)):
        piece = lax.dynamic_index_in_dim(parts, lax.rem(me + d, length), 0, keepdims=False)
        total = total + lax.ppermute(piece, axis, [(i, (i + d) % length) for i in range(length)])
    return total


def gather_pairs(x, axis):
    length = lax.axis_size(axis)
    chips = length // 2
    groups = [[2 * i + c for i in range(chips)] for c in range(2)]
    spread = jnp.broadcast_to(x[None], (chips, *x.shape))
    mine = lax.all_to_all(spread, axis, 0, 0, axis_index_groups=groups, tiled=True)
    theirs = lax.ppermute(mine, axis, [(i, i ^ 1) for i in range(length)])
    first = lax.rem(lax.axis_index(axis), 2) == 0
    pairs = jnp.stack([jnp.where(first, mine, theirs), jnp.where(first, theirs, mine)], axis=1)
    return pairs.reshape(length * x.shape[0], *x.shape[1:])


def sum_of_four(x, axis):
    other = [lax.ppermute(x, axis, [(i, i ^ d) for i in range(4)]) for d in (1, 2, 3)]
    return (x + other[0]) + (other[1] + other[2])


def per_device(
    activations, out_grads, proj_in, proj_out, lengths, example_ids, prior_cov, damping, queries
):
    ex_local = lengths.shape[0]
    seq_len = activations.shape[1] // ex_local
    tokens = activations.shape[1]
    proj_size = KP * KP
    n_query = queries.shape[1]
    live_mask = (jnp.arange(seq_len, dtype=jnp.int32)[None, :] < lengths[:, None]).astype(
        jnp.float32
    )
    in_parts = jnp.einsum("ltf,lkf->ltk", activations, proj_in, preferred_element_type=jnp.float32)
    out_parts = jnp.einsum("ltf,lkf->ltk", out_grads, proj_out, preferred_element_type=jnp.float32)
    owned = to_layer(jnp.concatenate([in_parts, out_parts], axis=1), "tensor")
    in_rows = owned[:tokens].reshape(ex_local, seq_len, KP) * live_mask[:, :, None]
    out_rows = owned[tokens:].reshape(ex_local, seq_len, KP)
    proj_grads = jnp.einsum(
        "est,esu->etu", out_rows, in_rows, precision=lax.Precision.HIGHEST
    ).reshape(ex_local, proj_size)
    sent = jnp.concatenate([proj_grads, example_ids.astype(jnp.float32)[:, None]], axis=1)
    gathered = gather_pairs(sent, "dp")
    grads = gathered[:, :proj_size]
    ids = gathered[:, proj_size].astype(jnp.int32)
    mine = lax.axis_index("dp") * ex_local + jnp.arange(ex_local, dtype=jnp.int32)
    pick = (ids[None, :] == mine[:, None]).astype(jnp.float32)
    picked = jnp.dot(pick, grads, precision=lax.Precision.HIGHEST)
    right = jnp.concatenate(
        [queries[0], picked, jnp.zeros((B - n_query - ex_local, proj_size), jnp.float32)], axis=0
    )
    product = scores_of(prior_cov[0], damping, grads, right)
    layer_scores = product[n_query : n_query + ex_local, :n_query]
    return sum_of_four(layer_scores, "tensor")


def solution(mesh):
    in_specs = (
        P(None, "dp", "tensor"),
        P(None, "dp", "tensor"),
        P(None, None, "tensor"),
        P(None, None, "tensor"),
        P("dp"),
        P("dp"),
        P("tensor", None, None),
        P("tensor"),
        P("tensor", None, None),
    )
    out_specs = P("dp", None)
    return jax.shard_map(
        per_device, mesh=mesh, in_specs=in_specs, out_specs=out_specs, check_vma=False
    )
```

time: 196 us -> 121 us (0.62)
  Pallas kernels: 126 us -> 63 us
  blocking collectives: 35.7 us -> 17.3 us
  starting transfers between devices: 4.57 us -> 9.21 us
    pallas_call x1, Pallas kernels: 126 us -> 63 us  [scores_of(): pl.pallas_call(solve_kernel, out_shape=jax.ShapeDtypeStruct((B, B), jnp.f...]
    all_gather x1 -> x0, blocking collectives: 26.2 us -> none  [per_device(): gathered = lax.all_gather(sent, 'dp', axis=0, tiled=True)]
    all_to_all x0 -> x1, blocking collectives: none -> 17.3 us  [gather_pairs(): lax.all_to_all(spread, axis, 0, 0, axis_index_groups=groups, tiled=True)]
    ppermute x0 -> x7, waiting for transfers between devices: none -> 11.1 us  [the longest x3 6.5 us: to_layer(): lax.ppermute(piece, axis, [(i, (i + d) % length) for i in range(length)])]
    all_to_all x1 -> x0, waiting for transfers between devices: 9.96 us -> none  [sent_and_summed(): pieces = lax.all_to_all(cut_along(x, dim, length), axis, 0, 0, tiled=True)]
    psum x1 -> x0, blocking collectives: 9.44 us -> none  [per_device(): return lax.psum(layer_scores, 'tensor')]
    ppermute x0 -> x7, starting transfers between devices: none -> 9.21 us  [the longest x3 5.4 us: to_layer(): lax.ppermute(piece, axis, [(i, (i + d) % length) for i in range(length)])]
    all_to_all x1 -> x0, starting transfers between devices: 4.57 us -> none  [sent_and_summed(): pieces = lax.all_to_all(cut_along(x, dim, length), axis, 0, 0, tiled=True)]
  transfers between devices with their start and end apart: 1 -> 7, of which waited for: 1 -> 7; matrix products, arithmetic and copies ran while one was open for 0% -> 0% of each run, Pallas kernels for 0% -> 0%
where the time goes in v2:
time: 121 us
  Pallas kernels  63 us (52%)
  blocking collectives  17.3 us (14%)
  matrix products  13.8 us (11%)
  waiting for transfers between devices  11.1 us (9%)
  starting transfers between devices  9.21 us (8%)
  other arithmetic  3.08 us (3%)
  local copies, waits for them, and re-layouts  2.65 us (2%)
    pallas_call x1, Pallas kernels, scores_of(): pl.pallas_call(solve_kernel, out_shape=jax.ShapeDtypeStruct((B, B), jnp.f...  63 us
    all_to_all x1, blocking collectives, gather_pairs(): lax.all_to_all(spread, axis, 0, 0, axis_index_groups=groups, tiled=True)  17.3 us
    dot_general x1, matrix products, per_device(): jnp.einsum('ltf,lkf->ltk', activations, proj_in, preferred_element_type=j...  9.55 us
    ppermute x3, waiting for transfers between devices, to_layer(): lax.ppermute(piece, axis, [(i, (i + d) % length) for i in range(length)])  6.5 us
    ppermute x3, starting transfers between devices, to_layer(): lax.ppermute(piece, axis, [(i, (i + d) % length) for i in range(length)])  5.4 us
    ppermute x3, starting transfers between devices, sum_of_four(): lax.ppermute(x, axis, [(i, i ^ d) for i in range(4)])  3.81 us
    ppermute x3, waiting for transfers between devices, sum_of_four(): lax.ppermute(x, axis, [(i, i ^ d) for i in range(4)])  3.58 us
    dot_general x1, matrix products, per_device(): jnp.einsum('ltf,lkf->ltk', out_grads, proj_out, preferred_element_type=jn...  3.55 us
  transfers between devices with their start and end apart: 7, of which 7 were waited for; matrix products, arithmetic and copies ran while one was open for 0% of the time, Pallas kernels for 0%

profile of v2, /device:TPU:0, one launch (start us, length us, event | category | flops | bytes accessed | tf_op | source)
XLA Modules:
  0.0 120.9 jit_solution(6611708889126764065)
XLA Ops:
  0.0 0.0 copy-start
  0.0 1.3 %copy-done = bf16[4,40,3584]{2,1,0:T(8,128)(2,1)S(1)} copy-done((bf16[4,40,3584]{2,1,0:T(8,128)(2,1)S(1)}, bf16[4,40,3584]{2,1,0:T(8,128)(2,1)}, u32[]{:S(2)}) %copy-start) | copy-done | bytes 1146904
  1.3 0.0 copy-start.3
  1.3 9.6 %fusion.23 = f32[4,512,40]{1,2,0:T(8,128)S(1)} fusion(bf16[4,512,3584]{2,1,0:T(8,128)(2,1)} %param.9, bf16[4,40,3584]{2,1,0:T(8,128)(2,1)S(1)} %copy-done), kind=kOutput, calls=%fused_computation.43 | convolution fusion | flops 587202560 | bytes 16154624 | tf_op jit(solution)/shard_map/ltf,lkf->ltk/dot_general | solution.py:204
  10.8 0.0 copy-done.3
  10.8 0.0 copy-start.5
  10.9 0.0 copy-start.4
  10.9 3.6 %fusion.24 = f32[4,512,40]{1,2,0:T(8,128)S(1)} fusion(bf16[4,512,1024]{2,1,0:T(8,128)(2,1)} %param.10, bf16[4,40,1024]{2,1,0:T(8,128)(2,1)S(1)} %copy-done.3), kind=kOutput, calls=%fused_computation.44 | convolution fusion | flops 167772160 | bytes 4849664 | tf_op jit(solution)/shard_map/ltf,lkf->ltk/dot_general | solution.py:205
  14.5 1.8 %collective-permute-start = (f32[1024,40]{0,1:T(8,128)S(1)}, f32[1024,40]{0,1:T(8,128)S(1)}, u32[]{:S(2)}, u32[]{:S(2)}) collective-permute-start(f32[1024,40]{0,1:T(8,128)S(1)} %get-tuple-element.7), channel_id=1, source_target_pairs={{0,1},{1,2},{2,3},{3,0},{4,5},{5,6},{6,7},{7,4},{8,9},{9,10},{10,1... | collective-permute-start | bytes 491528 | tf_op jit(solution)/shard_map/ppermute | solution.py:172
  16.2 1.5 %collective-permute-start.1 = (f32[1024,40]{0,1:T(8,128)S(1)}, f32[1024,40]{0,1:T(8,128)S(1)}, u32[]{:S(2)}, u32[]{:S(2)}) collective-permute-start(f32[1024,40]{0,1:T(8,128)S(1)} %get-tuple-element.8), channel_id=1, source_target_pairs={{0,3},{1,0},{2,1},{3,2},{4,7},{5,4},{6,5},{7,6},{8,11},{9,8},{10,9... | collective-permute-start | bytes 491528 | tf_op jit(solution)/shard_map/ppermute | solution.py:172
  17.8 2.1 %collective-permute-start.2 = (f32[1024,40]{0,1:T(8,128)S(1)}, f32[1024,40]{0,1:T(8,128)S(1)}, u32[]{:S(2)}, u32[]{:S(2)}) collective-permute-start(f32[1024,40]{0,1:T(8,128)S(1)} %get-tuple-element.9), channel_id=1, source_target_pairs={{0,2},{1,3},{2,0},{3,1},{4,6},{5,7},{6,4},{7,5},{8,10},{9,11},{10,... | collective-permute-start | bytes 491528 | tf_op jit(solution)/shard_map/ppermute | solution.py:172
  19.9 0.0 copy-done.5
  19.9 0.1 copy.14
  20.0 0.0 copy-done.4
  20.0 0.1 fusion.16
  20.1 1.8 %collective-permute-done = f32[1024,40]{0,1:T(8,128)S(1)} collective-permute-done((f32[1024,40]{0,1:T(8,128)S(1)}, f32[1024,40]{0,1:T(8,128)S(1)}, u32[]{:S(2)}, u32[]{:S(2)}) %collective-permute-start) | collective-permute-done | bytes 163872 | tf_op jit(solution)/shard_map/ppermute | solution.py:172
  21.9 2.9 %collective-permute-done.1 = f32[1024,40]{0,1:T(8,128)S(1)} collective-permute-done((f32[1024,40]{0,1:T(8,128)S(1)}, f32[1024,40]{0,1:T(8,128)S(1)}, u32[]{:S(2)}, u32[]{:S(2)}) %collective-permute-start.1) | collective-permute-done | bytes 163872 | tf_op jit(solution)/shard_map/ppermute | solution.py:172
  24.8 1.8 %collective-permute-done.2 = f32[1024,40]{0,1:T(8,128)S(1)} collective-permute-done((f32[1024,40]{0,1:T(8,128)S(1)}, f32[1024,40]{0,1:T(8,128)S(1)}, u32[]{:S(2)}, u32[]{:S(2)}) %collective-permute-start.2) | collective-permute-done | bytes 163872 | tf_op jit(solution)/shard_map/ppermute | solution.py:172
  26.6 0.0 copy-start.2
  26.7 0.3 fusion.11
  27.0 0.1 reshape.47
  27.1 0.1 pad_maximum_fusion.1
  27.2 0.1 broadcast_in_dim.7
  27.2 17.3 %all_to_all.5 = f32[16,4,1601]{2,1,0:T(4,128)S(1)} all-to-all(f32[16,4,1601]{2,1,0:T(4,128)S(1)} %broadcast_in_dim.7), channel_id=1, replica_groups={{0,8,16,24,32,40,48,56,64,72,80,88,96,104,112,120},{4,12,20,28,36,44,52..., dimensions={0} | all-to-all | bytes 819712 | tf_op jit(solution)/shard_map/all_to_all | solution.py:181
  44.5 0.0 collective-permute-start.3
  45.2 0.1 pad.2.clone
  45.2 1.0 collective-permute-done.3
  46.3 0.1 select_bitcast_fusion.1
  46.4 0.2 pad_maximum_fusion
  46.6 0.3 reshape.48
  46.9 0.0 copy-start.1
  46.9 0.2 fusion.15
  47.1 0.4 fusion.17
  47.5 0.0 copy-done.2
  47.5 1.1 maximum_maximum_fusion.right_ref
  48.6 0.0 copy-done.1
  48.6 63.0 %shard_map.91 = f32[128,128]{1,0:T(8,128)} custom-call(bf16[1600,1600]{1,0:T(8,128)(2,1)} %bitcast.40, f32[1]{0:T(128)S(6)} %copy.23.damp_ref, f32[128,1600]{1,0:T(8,128)} %bitcast.39, f32[128,1600]{1,0:T(8,128)} %maximum_maximum_fusion.right_ref), custom_call_target="tpu_custom_call" | custom-call | tf_op jit(solution)/shard_map/pallas_call | solution.py:152
  111.6 0.7 slice.24
  112.3 0.7 collective-permute-start.5
  113.0 3.1 %collective-permute-start.6 = (f32[4,64]{1,0:T(4,128)S(1)}, f32[4,64]{1,0:T(4,128)S(1)}, u32[]{:S(2)}, u32[]{:S(2)}) collective-permute-start(f32[4,64]{1,0:T(4,128)S(1)} %slice.24), channel_id=1, source_target_pairs={{0,3},{1,2},{2,1},{3,0},{4,7},{5,6},{6,5},{7,4},{8,11},{9,10},{10,... | collective-permute-start | bytes 3080 | tf_op jit(solution)/shard_map/ppermute | solution.py:189
  116.1 0.0 collective-permute-start.4
  116.1 1.3 %collective-permute-done.5 = f32[4,64]{1,0:T(4,128)S(1)} collective-permute-done((f32[4,64]{1,0:T(4,128)S(1)}, f32[4,64]{1,0:T(4,128)S(1)}, u32[]{:S(2)}, u32[]{:S(2)}) %collective-permute-start.5) | collective-permute-done | bytes 1056 | tf_op jit(solution)/shard_map/ppermute | solution.py:189
  117.3 0.4 collective-permute-done.6
  117.8 1.9 %collective-permute-done.4 = f32[4,64]{1,0:T(4,128)S(1)} collective-permute-done((f32[4,64]{1,0:T(4,128)S(1)}, f32[4,64]{1,0:T(4,128)S(1)}, u32[]{:S(2)}, u32[]{:S(2)}) %collective-permute-start.4) | collective-permute-done | bytes 1056 | tf_op jit(solution)/shard_map/ppermute | solution.py:189
  119.6 1.3 %add_add_fusion = f32[4,64]{1,0:T(4,128)} fusion(f32[4,64]{1,0:T(4,128)S(1)} %collective-permute-done.5, f32[4,64]{1,0:T(4,128)S(1)} %collective-permute-done.6, f32[4,64]{1,0:T(4,128)S(1)} %collective-permute-done.4, f32[128,128]{1,0:T(8,128)} %shard_map.91), kind=kLoop, calls=%fused_computation.32 | loop fusion | flops 768 | bytes 5120 | tf_op jit(solution)/shard_map/add | solution.py:190
  (9 shorter events, 0.1 us)
Async XLA Ops:
  0.0 1.3 %copy-start = (bf16[4,40,3584]{2,1,0:T(8,128)(2,1)S(1)}, bf16[4,40,3584]{2,1,0:T(8,128)(2,1)}, u32[]{:S(2)}) copy-start(bf16[4,40,3584]{2,1,0:T(8,128)(2,1)} %param.11) | copy-start | bytes 3440644
  1.3 9.6 %copy-start.3 = (bf16[4,40,1024]{2,1,0:T(8,128)(2,1)S(1)}, bf16[4,40,1024]{2,1,0:T(8,128)(2,1)}, u32[]{:S(2)}) copy-start(bf16[4,40,1024]{2,1,0:T(8,128)(2,1)} %param.12) | copy-start | bytes 983044
  10.8 9.0 %copy-start.5 = (s32[4]{0:T(128)S(1)}, s32[4]{0:T(128)}, u32[]{:S(2)}) copy-start(s32[4]{0:T(128)} %param.14) | copy-start | bytes 52
  10.9 9.1 %copy-start.4 = (s32[4]{0:T(128)S(1)}, s32[4]{0:T(128)}, u32[]{:S(2)}) copy-start(s32[4]{0:T(128)} %param.13) | copy-start | bytes 52
  14.5 7.4 %collective-permute-start = (f32[1024,40]{0,1:T(8,128)S(1)}, f32[1024,40]{0,1:T(8,128)S(1)}, u32[]{:S(2)}, u32[]{:S(2)}) collective-permute-start(f32[1024,40]{0,1:T(8,128)S(1)} %get-tuple-element.7), channel_id=1, source_target_pairs={{0,1},{1,2},{2,3},{3,0},{4,5},{5,6},{6,7},{7,4},{8,9},{9,10},{10,1... | collective-permute-start | bytes 491528 | tf_op jit(solution)/shard_map/ppermute | solution.py:172
  16.2 8.5 %collective-permute-start.1 = (f32[1024,40]{0,1:T(8,128)S(1)}, f32[1024,40]{0,1:T(8,128)S(1)}, u32[]{:S(2)}, u32[]{:S(2)}) collective-permute-start(f32[1024,40]{0,1:T(8,128)S(1)} %get-tuple-element.8), channel_id=1, source_target_pairs={{0,3},{1,0},{2,1},{3,2},{4,7},{5,4},{6,5},{7,6},{8,11},{9,8},{10,9... | collective-permute-start | bytes 491528 | tf_op jit(solution)/shard_map/ppermute | solution.py:172
  17.8 8.8 %collective-permute-start.2 = (f32[1024,40]{0,1:T(8,128)S(1)}, f32[1024,40]{0,1:T(8,128)S(1)}, u32[]{:S(2)}, u32[]{:S(2)}) collective-permute-start(f32[1024,40]{0,1:T(8,128)S(1)} %get-tuple-element.9), channel_id=1, source_target_pairs={{0,2},{1,3},{2,0},{3,1},{4,6},{5,7},{6,4},{7,5},{8,10},{9,11},{10,... | collective-permute-start | bytes 491528 | tf_op jit(solution)/shard_map/ppermute | solution.py:172
  26.6 20.9 %copy-start.2 = (f32[1,64,1600]{2,1,0:T(8,128)S(1)}, f32[1,64,1600]{2,1,0:T(8,128)}, u32[]{:S(2)}) copy-start(f32[1,64,1600]{2,1,0:T(8,128)} %param.17) | copy-start | bytes 1228804
  44.5 1.8 %collective-permute-start.3 = (f32[16,4,1601]{2,1,0:T(4,128)S(1)}, f32[16,4,1601]{2,1,0:T(4,128)S(1)}, u32[]{:S(2)}, u32[]{:S(2)}) collective-permute-start(f32[16,4,1601]{2,1,0:T(4,128)S(1)} %all_to_all.5), channel_id=1, source_target_pairs={{0,4},{4,0},{8,12},{12,8},{16,20},{20,16},{24,28},{28,24},{32,36},... | collective-permute-start | bytes 1229576 | tf_op jit(solution)/shard_map/ppermute | solution.py:182
  46.9 1.7 %copy-start.1 = (f32[128,1601]{1,0:T(8,128)}, f32[128,1601]{1,0:T(8,128)S(1)}, u32[]{:S(2)}) copy-start(f32[128,1601]{1,0:T(8,128)S(1)} %reshape.48) | copy-start | bytes 2459140
  112.3 5.1 %collective-permute-start.5 = (f32[4,64]{1,0:T(4,128)S(1)}, f32[4,64]{1,0:T(4,128)S(1)}, u32[]{:S(2)}, u32[]{:S(2)}) collective-permute-start(f32[4,64]{1,0:T(4,128)S(1)} %slice.24), channel_id=1, source_target_pairs={{0,2},{1,3},{2,0},{3,1},{4,6},{5,7},{6,4},{7,5},{8,10},{9,11},{10,... | collective-permute-start | bytes 3080 | tf_op jit(solution)/shard_map/ppermute | solution.py:189
  113.0 4.8 %collective-permute-start.6 = (f32[4,64]{1,0:T(4,128)S(1)}, f32[4,64]{1,0:T(4,128)S(1)}, u32[]{:S(2)}, u32[]{:S(2)}) collective-permute-start(f32[4,64]{1,0:T(4,128)S(1)} %slice.24), channel_id=1, source_target_pairs={{0,3},{1,2},{2,1},{3,0},{4,7},{5,6},{6,5},{7,4},{8,11},{9,10},{10,... | collective-permute-start | bytes 3080 | tf_op jit(solution)/shard_map/ppermute | solution.py:189
  116.1 3.6 %collective-permute-start.4 = (f32[4,64]{1,0:T(4,128)S(1)}, f32[4,64]{1,0:T(4,128)S(1)}, u32[]{:S(2)}, u32[]{:S(2)}) collective-permute-start(f32[4,64]{1,0:T(4,128)S(1)} %slice.24), channel_id=1, source_target_pairs={{0,1},{1,0},{2,3},{3,2},{4,5},{5,4},{6,7},{7,6},{8,9},{9,8},{10,11... | collective-permute-start | bytes 3080 | tf_op jit(solution)/shard_map/ppermute | solution.py:189

commit v3 on v2

--- a/solution.py
+++ b/solution.py
@@ -21,7 +21,7 @@
     return jnp.broadcast_to(row, (8, B))
 
 
-def block_inverse(block):
+def block_inverse(block, groups, beside):
     lane = lax.broadcasted_iota(jnp.int32, (8, B), 1)
     sub = lax.broadcasted_iota(jnp.int32, (8, B), 0)
     rows = [block[8 * h : 8 * h + 8] for h in range(16)]
@@ -29,12 +29,12 @@
     def columns(piece, first):
         return [jnp.broadcast_to(piece[:, first + m : first + m + 1], (8, B)) for m in range(S)]
 
-    for g in range(B // S):
+    for g in range(groups):
         first = S * g
         here = (2 * g, 2 * g + 1)
         in_pivot = (lane >= first) & (lane < first + S)
         cols = [list(pair) for pair in zip(*(columns(rows[h], first) for h in here))]
-        after = (2 * g + 2, 2 * g + 3) if g + 1 < B // S else ()
+        after = (2 * g + 2, 2 * g + 3) if g + 1 < groups else ()
         next_cols = [columns(rows[h], first) for h in after]
         panel = [
             jnp.where(in_pivot, jnp.where(lane - first == sub + 8 * q, 1.0, 0.0), rows[h])
@@ -74,14 +74,17 @@
             else:
                 fresh.append(kept - change[8 * h : 8 * h + 8])
         rows = fresh
+        beside(g)
     return jnp.concatenate(rows, axis=0)
 
 
-def solve_kernel(prior_ref, damp_ref, grads_ref, right_ref, out_ref, work, left, terms):
+def solve_kernel(prior_ref, damp_ref, first_ref, slots_ref, queries_ref, out_ref, work, left, terms):
     size = prior_ref.shape[0]
     blocks = pl.cdiv(size, B)
     tail = blocks * B
-    examples = grads_ref.shape[0]
+    examples = slots_ref.shape[0]
+    n_query = queries_ref.shape[0]
+    n_own = out_ref.shape[0]
     whole = size // B * B
     r = lax.broadcasted_iota(jnp.int32, (B, B), 0)
     c = lax.broadcasted_iota(jnp.int32, (B, B), 1)
@@ -106,61 +109,79 @@
             work[here, here.stop : (k + 1) * B] = jnp.zeros((size - k * B, (k + 1) * B - size), jnp.float32)
         spot = slice(k * B, (k + 1) * B)
         work[spot, spot] += jnp.where(r == c, jnp.where(r + k * B < size, damp_ref[0], 1.0), 0.0)
-    work[tail : tail + B, 0:size] = right_ref[...]
+    slots = jnp.concatenate(
+        [slots_ref[...], jnp.zeros((examples, tail - slots_ref.shape[1]), jnp.float32)], axis=1
+    )
+    slots_t = slots.T
+    grads = slots[:, :size]
+    grads_t = slots_t[:size]
+    ids = jnp.broadcast_to(slots_t[size : size + 1].astype(jnp.int32), (B - n_query, examples))
+    row = lax.broadcasted_iota(jnp.int32, (B - n_query, examples), 0)
+    pick = jnp.where((ids == row + first_ref[0]) & (row < n_own), 1.0, 0.0)
+    work[tail : tail + n_query, 0:size] = queries_ref[...]
+    work[tail + n_query : tail + B, 0:size] = jnp.dot(
+        pick, grads, preferred_element_type=jnp.float32, precision=lax.Precision.HIGHEST
+    )
     work[tail : tail + B, size:tail] = jnp.zeros((B, tail - size), jnp.float32)
     work[tail : tail + B, tail : tail + B] = jnp.zeros((B, B), jnp.float32)
-    left[...] = jnp.zeros_like(left)
-    terms[...] = jnp.zeros_like(terms)
-    grads_t = grads_ref[...].T
+    for ref in (left, terms):
+        ref[size:, :] = jnp.zeros((ref.shape[0] - size, ref.shape[1]), ref.dtype)
     set_left(slice(0, size), grads_t)
     set_terms(slice(0, size), grads_t * (-1.0 / examples))
 
     def product(x, y):
         return lax.dot_general(x, y, (((1,), (1,)), ((), ())), preferred_element_type=jnp.float32)
 
-    def step(k, count):
+    def step(k, count, groups):
         def at(t, n=1):
             return pl.ds(pl.multiple_of((k + t) * B, B), n * B)
 
-        inverse = block_inverse(work[at(0), at(0)] - product(left[at(0), :], terms[at(0), :]))
-        for t in range(0, count, 2):
-            n = min(2, count - t)
-            rows = at(t, count - t)
-            work[rows, at(t, n)] -= product(left[rows, :], terms[at(t, n), :])
+        def beside(g):
+            t = 2 * g
+            if t < count:
+                n = min(2, count - t)
+                rows = at(t, count - t)
+                work[rows, at(t, n)] -= product(left[rows, :], terms[at(t, n), :])
+
+        block = work[at(0), at(0)] - product(left[at(0), :], terms[at(0), :])
+        inverse = block_inverse(block, groups, beside)
         rows = at(1, count - 1)
         set_left(rows, work[rows, at(0)])
         high, low = split(inverse)
         stacked = jnp.concatenate([high, low, high], axis=0)
         set_terms(rows, jnp.dot(left[rows, :], stacked, preferred_element_type=jnp.float32))
 
-    for start, stop in zip(STARTS, (*STARTS[1:], blocks)):
+    for start, stop in zip(STARTS, (*STARTS[1:], blocks - 1)):
 
         def body(k, carry, count=blocks + 1 - start):
-            step(k, count)
+            step(k, count, B // S)
             return carry
 
         lax.fori_loop(start, stop, body, 0)
+    step(blocks - 1, 2, pl.cdiv(size - (blocks - 1) * B, S))
     last = slice(tail, tail + B)
-    out_ref[...] = product(left[last, :], terms[last, :]) - work[last, last]
-
-
-def scores_of(prior, damping, grads, right):
+    result = product(left[last, :], terms[last, :]) - work[last, last]
+    out_ref[...] = result[n_query : n_query + n_own, :n_query]
+
+
+def scores_of(prior, damping, first, slots, queries, own):
     blocks = pl.cdiv(prior.shape[0], B)
-    most = max(b - a for a, b in zip(STARTS, (*STARTS[1:], blocks)))
+    most = max(b - a for a, b in zip(STARTS, (*STARTS[1:], blocks - 1)))
     width = (blocks + most) * B
     vmem = pl.BlockSpec(memory_space=pltpu.VMEM)
+    smem = pl.BlockSpec(memory_space=pltpu.SMEM)
     return pl.pallas_call(
         solve_kernel,
-        out_shape=jax.ShapeDtypeStruct((B, B), jnp.float32),
-        in_specs=[vmem, pl.BlockSpec(memory_space=pltpu.SMEM), vmem, vmem],
+        out_shape=jax.ShapeDtypeStruct((own, queries.shape[0]), jnp.float32),
+        in_specs=[vmem, smem, smem, vmem, vmem],
         out_specs=vmem,
         scratch_shapes=[
             pltpu.VMEM((width, width), jnp.float32),
             pltpu.VMEM((width, 3 * B), jnp.bfloat16),
             pltpu.VMEM((width, 3 * B), jnp.bfloat16),
         ],
-        compiler_params=pltpu.CompilerParams(vmem_limit_bytes=60 * 2**20),
-    )(prior, damping, grads, right)
+        compiler_params=pltpu.CompilerParams(vmem_limit_bytes=36 * 2**20),
+    )(prior, damping, first, slots, queries)
 
 
 def to_layer(parts, axis):
@@ -197,7 +218,6 @@
     seq_len = activations.shape[1] // ex_local
     tokens = activations.shape[1]
     proj_size = KP * KP
-    n_query = queries.shape[1]
     live_mask = (jnp.arange(seq_len, dtype=jnp.int32)[None, :] < lengths[:, None]).astype(
         jnp.float32
     )
@@ -211,16 +231,8 @@
     ).reshape(ex_local, proj_size)
     sent = jnp.concatenate([proj_grads, example_ids.astype(jnp.float32)[:, None]], axis=1)
     gathered = gather_pairs(sent, "dp")
-    grads = gathered[:, :proj_size]
-    ids = gathered[:, proj_size].astype(jnp.int32)
-    mine = lax.axis_index("dp") * ex_local + jnp.arange(ex_local, dtype=jnp.int32)
-    pick = (ids[None, :] == mine[:, None]).astype(jnp.float32)
-    picked = jnp.dot(pick, grads, precision=lax.Precision.HIGHEST)
-    right = jnp.concatenate(
-        [queries[0], picked, jnp.zeros((B - n_query - ex_local, proj_size), jnp.float32)], axis=0
-    )
-    product = scores_of(prior_cov[0], damping, grads, right)
-    layer_scores = product[n_query : n_query + ex_local, :n_query]
+    first = (lax.axis_index("dp") * ex_local).astype(jnp.int32)[None]
+    layer_scores = scores_of(prior_cov[0], damping, first, gathered, queries[0], ex_local)
     return sum_of_four(layer_scores, "tensor")
 
 

time: 121 us -> 107 us (0.88)
  Pallas kernels: 63 us -> 48.7 us
  other arithmetic: 3.08 us -> 1.16 us
  local copies, waits for them, and re-layouts: 2.65 us -> 4.39 us
    pallas_call x1, Pallas kernels: 63 us -> 48.7 us  [scores_of(): pl.pallas_call(solve_kernel, out_shape=jax.ShapeDtypeStruct((own, queries...]
    unnamed x13, local copies, waits for them, and re-layouts: 1.3 us -> 3.8 us
  transfers between devices with their start and end apart: 7 -> 7, of which waited for: 7 -> 6; matrix products, arithmetic and copies ran while one was open for 0% -> 0% of each run, Pallas kernels for 0% -> 0%
where the time goes in v3:
time: 107 us
  Pallas kernels  48.7 us (46%)
  blocking collectives  17.3 us (16%)
  matrix products  13.4 us (13%)
  waiting for transfers between devices  11 us (10%)
  starting transfers between devices  10.2 us (10%)
  local copies, waits for them, and re-layouts  4.39 us (4%)
  other arithmetic  1.16 us (1%)
    pallas_call x1, Pallas kernels, scores_of(): pl.pallas_call(solve_kernel, out_shape=jax.ShapeDtypeStruct((own, queries...  48.7 us
    all_to_all x1, blocking collectives, gather_pairs(): lax.all_to_all(spread, axis, 0, 0, axis_index_groups=groups, tiled=True)  17.3 us
    dot_general x1, matrix products, per_device(): jnp.einsum('ltf,lkf->ltk', activations, proj_in, preferred_element_type=j...  9.55 us
    ppermute x3, waiting for transfers between devices, to_layer(): lax.ppermute(piece, axis, [(i, (i + d) % length) for i in range(length)])  6.5 us
    ppermute x3, starting transfers between devices, to_layer(): lax.ppermute(piece, axis, [(i, (i + d) % length) for i in range(length)])  5.4 us
    ppermute x3, starting transfers between devices, sum_of_four(): lax.ppermute(x, axis, [(i, i ^ d) for i in range(4)])  4.78 us
    unnamed x13, local copies, waits for them, and re-layouts  3.8 us
    dot_general x1, matrix products, per_device(): jnp.einsum('ltf,lkf->ltk', out_grads, proj_out, preferred_element_type=jn...  3.55 us
  transfers between devices with their start and end apart: 7, of which 6 were waited for; matrix products, arithmetic and copies ran while one was open for 0% of the time, Pallas kernels for 0%

profile of v3, /device:TPU:0, one launch (start us, length us, event | category | flops | bytes accessed | tf_op | source)
XLA Modules:
  0.0 106.9 jit_solution(14638732764327849655)
XLA Ops:
  0.0 0.0 copy-start
  0.0 1.3 %copy-done = bf16[4,40,3584]{2,1,0:T(8,128)(2,1)S(1)} copy-done((bf16[4,40,3584]{2,1,0:T(8,128)(2,1)S(1)}, bf16[4,40,3584]{2,1,0:T(8,128)(2,1)}, u32[]{:S(2)}) %copy-start) | copy-done | bytes 1146904
  1.3 0.0 copy-start.3
  1.3 9.6 %fusion.17 = f32[4,512,40]{1,2,0:T(8,128)S(1)} fusion(bf16[4,512,3584]{2,1,0:T(8,128)(2,1)} %param.9, bf16[4,40,3584]{2,1,0:T(8,128)(2,1)S(1)} %copy-done), kind=kOutput, calls=%fused_computation.34 | convolution fusion | flops 587202560 | bytes 16154624 | tf_op jit(solution)/shard_map/ltf,lkf->ltk/dot_general | solution.py:224
  10.8 0.0 copy-done.3
  10.8 0.0 copy-start.5
  10.9 0.0 copy-start.4
  10.9 3.6 %fusion.18 = f32[4,512,40]{1,2,0:T(8,128)S(1)} fusion(bf16[4,512,1024]{2,1,0:T(8,128)(2,1)} %param.10, bf16[4,40,1024]{2,1,0:T(8,128)(2,1)S(1)} %copy-done.3), kind=kOutput, calls=%fused_computation.35 | convolution fusion | flops 167772160 | bytes 4849664 | tf_op jit(solution)/shard_map/ltf,lkf->ltk/dot_general | solution.py:225
  14.5 1.8 %collective-permute-start = (f32[1024,40]{0,1:T(8,128)S(1)}, f32[1024,40]{0,1:T(8,128)S(1)}, u32[]{:S(2)}, u32[]{:S(2)}) collective-permute-start(f32[1024,40]{0,1:T(8,128)S(1)} %get-tuple-element.7), channel_id=1, source_target_pairs={{0,1},{1,2},{2,3},{3,0},{4,5},{5,6},{6,7},{7,4},{8,9},{9,10},{10,1... | collective-permute-start | bytes 491528 | tf_op jit(solution)/shard_map/ppermute | solution.py:193
  16.2 1.5 %collective-permute-start.1 = (f32[1024,40]{0,1:T(8,128)S(1)}, f32[1024,40]{0,1:T(8,128)S(1)}, u32[]{:S(2)}, u32[]{:S(2)}) collective-permute-start(f32[1024,40]{0,1:T(8,128)S(1)} %get-tuple-element.8), channel_id=1, source_target_pairs={{0,3},{1,0},{2,1},{3,2},{4,7},{5,4},{6,5},{7,6},{8,11},{9,8},{10,9... | collective-permute-start | bytes 491528 | tf_op jit(solution)/shard_map/ppermute | solution.py:193
  17.8 2.1 %collective-permute-start.2 = (f32[1024,40]{0,1:T(8,128)S(1)}, f32[1024,40]{0,1:T(8,128)S(1)}, u32[]{:S(2)}, u32[]{:S(2)}) collective-permute-start(f32[1024,40]{0,1:T(8,128)S(1)} %get-tuple-element.9), channel_id=1, source_target_pairs={{0,2},{1,3},{2,0},{3,1},{4,6},{5,7},{6,4},{7,5},{8,10},{9,11},{10,... | collective-permute-start | bytes 491528 | tf_op jit(solution)/shard_map/ppermute | solution.py:193
  19.9 0.0 copy-done.5
  19.9 0.1 copy.14
  20.0 0.0 copy-done.4
  20.0 0.1 fusion.15
  20.1 0.0 copy-start.2
  20.1 1.8 %collective-permute-done = f32[1024,40]{0,1:T(8,128)S(1)} collective-permute-done((f32[1024,40]{0,1:T(8,128)S(1)}, f32[1024,40]{0,1:T(8,128)S(1)}, u32[]{:S(2)}, u32[]{:S(2)}) %collective-permute-start) | collective-permute-done | bytes 163872 | tf_op jit(solution)/shard_map/ppermute | solution.py:193
  21.9 2.9 %collective-permute-done.1 = f32[1024,40]{0,1:T(8,128)S(1)} collective-permute-done((f32[1024,40]{0,1:T(8,128)S(1)}, f32[1024,40]{0,1:T(8,128)S(1)}, u32[]{:S(2)}, u32[]{:S(2)}) %collective-permute-start.1) | collective-permute-done | bytes 163872 | tf_op jit(solution)/shard_map/ppermute | solution.py:193
  24.8 1.8 %collective-permute-done.2 = f32[1024,40]{0,1:T(8,128)S(1)} collective-permute-done((f32[1024,40]{0,1:T(8,128)S(1)}, f32[1024,40]{0,1:T(8,128)S(1)}, u32[]{:S(2)}, u32[]{:S(2)}) %collective-permute-start.2) | collective-permute-done | bytes 163872 | tf_op jit(solution)/shard_map/ppermute | solution.py:193
  26.7 0.3 fusion.11
  27.0 0.1 reshape.37
  27.1 0.1 pad_maximum_fusion.1
  27.2 0.1 broadcast_in_dim.8
  27.2 17.3 %all_to_all.5 = f32[16,4,1601]{2,1,0:T(4,128)S(1)} all-to-all(f32[16,4,1601]{2,1,0:T(4,128)S(1)} %broadcast_in_dim.8), channel_id=1, replica_groups={{0,8,16,24,32,40,48,56,64,72,80,88,96,104,112,120},{4,12,20,28,36,44,52..., dimensions={0} | all-to-all | bytes 819712 | tf_op jit(solution)/shard_map/all_to_all | solution.py:202
  44.5 0.0 collective-permute-start.3
  45.1 1.1 %collective-permute-done.3 = f32[16,4,1601]{2,1,0:T(4,128)S(1)} collective-permute-done((f32[16,4,1601]{2,1,0:T(4,128)S(1)}, f32[16,4,1601]{2,1,0:T(4,128)S(1)}, u32[]{:S(2)}, u32[]{:S(2)}) %collective-permute-start.3) | collective-permute-done | bytes 409888 | tf_op jit(solution)/shard_map/ppermute | solution.py:203
  46.2 0.1 select_bitcast_fusion.1
  46.4 0.2 pad_maximum_fusion
  46.6 0.3 reshape.38.slots_ref
  46.9 0.0 copy-done.2
  46.9 0.0 copy-start.1
  46.9 2.5 %copy-done.1 = bf16[1,1600,1600]{2,1,0:T(8,128)(2,1)S(1)} copy-done((bf16[1,1600,1600]{2,1,0:T(8,128)(2,1)S(1)}, bf16[1,1600,1600]{2,1,0:T(8,128)(2,1)}, u32[]{:S(2)}) %copy-start.1) | copy-done | bytes 5120024
  49.4 48.7 %shard_map.91 = f32[4,64]{1,0:T(4,128)S(1)} custom-call(bf16[1600,1600]{1,0:T(8,128)(2,1)S(1)} %bitcast.39, f32[1]{0:T(128)S(6)} %copy.23.damp_ref, s32[1]{0:T(128)} %bitcast.1.first_ref, f32[128,1601]{1,0:T(8,128)S(1)} %reshape.38.slots_ref, f32[64,1600]{1,0:T(8,128)S(1)} %bitcast.40), custom_call_target="tpu_custom_call" | custom-call | tf_op jit(solution)/shard_map/pallas_call | solution.py:173
  98.1 1.2 %collective-permute-start.4 = (f32[4,64]{1,0:T(4,128)S(1)}, f32[4,64]{1,0:T(4,128)S(1)}, u32[]{:S(2)}, u32[]{:S(2)}) collective-permute-start(f32[4,64]{1,0:T(4,128)S(1)} %shard_map.91), channel_id=1, source_target_pairs={{0,1},{1,0},{2,3},{3,2},{4,5},{5,4},{6,7},{7,6},{8,9},{9,8},{10,11... | collective-permute-start | bytes 3080 | tf_op jit(solution)/shard_map/ppermute | solution.py:210
  99.3 2.2 %collective-permute-start.5 = (f32[4,64]{1,0:T(4,128)S(1)}, f32[4,64]{1,0:T(4,128)S(1)}, u32[]{:S(2)}, u32[]{:S(2)}) collective-permute-start(f32[4,64]{1,0:T(4,128)S(1)} %shard_map.91), channel_id=1, source_target_pairs={{0,2},{1,3},{2,0},{3,1},{4,6},{5,7},{6,4},{7,5},{8,10},{9,11},{10,... | collective-permute-start | bytes 3080 | tf_op jit(solution)/shard_map/ppermute | solution.py:210
  101.5 1.4 %collective-permute-start.6 = (f32[4,64]{1,0:T(4,128)S(1)}, f32[4,64]{1,0:T(4,128)S(1)}, u32[]{:S(2)}, u32[]{:S(2)}) collective-permute-start(f32[4,64]{1,0:T(4,128)S(1)} %shard_map.91), channel_id=1, source_target_pairs={{0,3},{1,2},{2,1},{3,0},{4,7},{5,6},{6,5},{7,4},{8,11},{9,10},{10,... | collective-permute-start | bytes 3080 | tf_op jit(solution)/shard_map/ppermute | solution.py:210
  102.9 0.0 collective-permute-done.4
  102.9 1.5 %collective-permute-done.5 = f32[4,64]{1,0:T(4,128)S(1)} collective-permute-done((f32[4,64]{1,0:T(4,128)S(1)}, f32[4,64]{1,0:T(4,128)S(1)}, u32[]{:S(2)}, u32[]{:S(2)}) %collective-permute-start.5) | collective-permute-done | bytes 1056 | tf_op jit(solution)/shard_map/ppermute | solution.py:210
  104.4 1.9 %collective-permute-done.6 = f32[4,64]{1,0:T(4,128)S(1)} collective-permute-done((f32[4,64]{1,0:T(4,128)S(1)}, f32[4,64]{1,0:T(4,128)S(1)}, u32[]{:S(2)}, u32[]{:S(2)}) %collective-permute-start.6) | collective-permute-done | bytes 1056 | tf_op jit(solution)/shard_map/ppermute | solution.py:210
  106.3 0.6 add_add_fusion
  (7 shorter events, 0.1 us)
Async XLA Ops:
  0.0 1.3 %copy-start = (bf16[4,40,3584]{2,1,0:T(8,128)(2,1)S(1)}, bf16[4,40,3584]{2,1,0:T(8,128)(2,1)}, u32[]{:S(2)}) copy-start(bf16[4,40,3584]{2,1,0:T(8,128)(2,1)} %param.11) | copy-start | bytes 3440644
  1.3 9.6 %copy-start.3 = (bf16[4,40,1024]{2,1,0:T(8,128)(2,1)S(1)}, bf16[4,40,1024]{2,1,0:T(8,128)(2,1)}, u32[]{:S(2)}) copy-start(bf16[4,40,1024]{2,1,0:T(8,128)(2,1)} %param.12) | copy-start | bytes 983044
  10.8 9.0 %copy-start.5 = (s32[4]{0:T(128)S(1)}, s32[4]{0:T(128)}, u32[]{:S(2)}) copy-start(s32[4]{0:T(128)} %param.14) | copy-start | bytes 52
  10.9 9.1 %copy-start.4 = (s32[4]{0:T(128)S(1)}, s32[4]{0:T(128)}, u32[]{:S(2)}) copy-start(s32[4]{0:T(128)} %param.13) | copy-start | bytes 52
  14.5 7.4 %collective-permute-start = (f32[1024,40]{0,1:T(8,128)S(1)}, f32[1024,40]{0,1:T(8,128)S(1)}, u32[]{:S(2)}, u32[]{:S(2)}) collective-permute-start(f32[1024,40]{0,1:T(8,128)S(1)} %get-tuple-element.7), channel_id=1, source_target_pairs={{0,1},{1,2},{2,3},{3,0},{4,5},{5,6},{6,7},{7,4},{8,9},{9,10},{10,1... | collective-permute-start | bytes 491528 | tf_op jit(solution)/shard_map/ppermute | solution.py:193
  16.2 8.5 %collective-permute-start.1 = (f32[1024,40]{0,1:T(8,128)S(1)}, f32[1024,40]{0,1:T(8,128)S(1)}, u32[]{:S(2)}, u32[]{:S(2)}) collective-permute-start(f32[1024,40]{0,1:T(8,128)S(1)} %get-tuple-element.8), channel_id=1, source_target_pairs={{0,3},{1,0},{2,1},{3,2},{4,7},{5,4},{6,5},{7,6},{8,11},{9,8},{10,9... | collective-permute-start | bytes 491528 | tf_op jit(solution)/shard_map/ppermute | solution.py:193
  17.8 8.8 %collective-permute-start.2 = (f32[1024,40]{0,1:T(8,128)S(1)}, f32[1024,40]{0,1:T(8,128)S(1)}, u32[]{:S(2)}, u32[]{:S(2)}) collective-permute-start(f32[1024,40]{0,1:T(8,128)S(1)} %get-tuple-element.9), channel_id=1, source_target_pairs={{0,2},{1,3},{2,0},{3,1},{4,6},{5,7},{6,4},{7,5},{8,10},{9,11},{10,... | collective-permute-start | bytes 491528 | tf_op jit(solution)/shard_map/ppermute | solution.py:193
  20.1 26.8 %copy-start.2 = (f32[1,64,1600]{2,1,0:T(8,128)S(1)}, f32[1,64,1600]{2,1,0:T(8,128)}, u32[]{:S(2)}) copy-start(f32[1,64,1600]{2,1,0:T(8,128)} %param.17) | copy-start | bytes 1228804
  44.5 1.8 %collective-permute-start.3 = (f32[16,4,1601]{2,1,0:T(4,128)S(1)}, f32[16,4,1601]{2,1,0:T(4,128)S(1)}, u32[]{:S(2)}, u32[]{:S(2)}) collective-permute-start(f32[16,4,1601]{2,1,0:T(4,128)S(1)} %all_to_all.5), channel_id=1, source_target_pairs={{0,4},{4,0},{8,12},{12,8},{16,20},{20,16},{24,28},{28,24},{32,36},... | collective-permute-start | bytes 1229576 | tf_op jit(solution)/shard_map/ppermute | solution.py:203
  46.9 2.5 %copy-start.1 = (bf16[1,1600,1600]{2,1,0:T(8,128)(2,1)S(1)}, bf16[1,1600,1600]{2,1,0:T(8,128)(2,1)}, u32[]{:S(2)}) copy-start(bf16[1,1600,1600]{2,1,0:T(8,128)(2,1)} %param.15) | copy-start | bytes 15360004
  98.1 4.8 %collective-permute-start.4 = (f32[4,64]{1,0:T(4,128)S(1)}, f32[4,64]{1,0:T(4,128)S(1)}, u32[]{:S(2)}, u32[]{:S(2)}) collective-permute-start(f32[4,64]{1,0:T(4,128)S(1)} %shard_map.91), channel_id=1, source_target_pairs={{0,1},{1,0},{2,3},{3,2},{4,5},{5,4},{6,7},{7,6},{8,9},{9,8},{10,11... | collective-permute-start | bytes 3080 | tf_op jit(solution)/shard_map/ppermute | solution.py:210
  99.3 5.1 %collective-permute-start.5 = (f32[4,64]{1,0:T(4,128)S(1)}, f32[4,64]{1,0:T(4,128)S(1)}, u32[]{:S(2)}, u32[]{:S(2)}) collective-permute-start(f32[4,64]{1,0:T(4,128)S(1)} %shard_map.91), channel_id=1, source_target_pairs={{0,2},{1,3},{2,0},{3,1},{4,6},{5,7},{6,4},{7,5},{8,10},{9,11},{10,... | collective-permute-start | bytes 3080 | tf_op jit(solution)/shard_map/ppermute | solution.py:210
  101.5 4.8 %collective-permute-start.6 = (f32[4,64]{1,0:T(4,128)S(1)}, f32[4,64]{1,0:T(4,128)S(1)}, u32[]{:S(2)}, u32[]{:S(2)}) collective-permute-start(f32[4,64]{1,0:T(4,128)S(1)} %shard_map.91), channel_id=1, source_target_pairs={{0,3},{1,2},{2,1},{3,0},{4,7},{5,6},{6,5},{7,4},{8,11},{9,10},{10,... | collective-permute-start | bytes 3080 | tf_op jit(solution)/shard_map/ppermute | solution.py:210

commit v4 on v3

--- a/solution.py
+++ b/solution.py
@@ -78,14 +78,22 @@
     return jnp.concatenate(rows, axis=0)
 
 
-def solve_kernel(prior_ref, damp_ref, first_ref, slots_ref, queries_ref, out_ref, work, left, terms):
+def solve_kernel(prior_ref, damp_ref, first_ref, slots_ref, queries_ref, out_ref, held, work, left, terms, sems):
     size = prior_ref.shape[0]
     blocks = pl.cdiv(size, B)
     tail = blocks * B
     examples = slots_ref.shape[0]
     n_query = queries_ref.shape[0]
     n_own = out_ref.shape[0]
-    whole = size // B * B
+    stripes = [slice(k * B, min((k + 1) * B, size)) for k in range(blocks)]
+    copies = [
+        pltpu.make_async_copy(
+            prior_ref.at[here, 0 : here.stop], held.at[here, 0 : here.stop], sems.at[k]
+        )
+        for k, here in enumerate(stripes)
+    ]
+    for copy in copies:
+        copy.start()
     r = lax.broadcasted_iota(jnp.int32, (B, B), 0)
     c = lax.broadcasted_iota(jnp.int32, (B, B), 1)
 
@@ -101,14 +109,6 @@
         terms[rows, B : 2 * B] = low
         terms[rows, 2 * B :] = high
 
-    for k in range(blocks):
-        here = slice(k * B, min((k + 1) * B, size))
-        work[here, 0 : here.stop] = prior_ref[here, 0 : here.stop].astype(jnp.float32)
-        if here.stop < (k + 1) * B:
-            work[here.stop : (k + 1) * B, 0 : (k + 1) * B] = jnp.zeros(((k + 1) * B - size, (k + 1) * B), jnp.float32)
-            work[here, here.stop : (k + 1) * B] = jnp.zeros((size - k * B, (k + 1) * B - size), jnp.float32)
-        spot = slice(k * B, (k + 1) * B)
-        work[spot, spot] += jnp.where(r == c, jnp.where(r + k * B < size, damp_ref[0], 1.0), 0.0)
     slots = jnp.concatenate(
         [slots_ref[...], jnp.zeros((examples, tail - slots_ref.shape[1]), jnp.float32)], axis=1
     )
@@ -129,6 +129,16 @@
     set_left(slice(0, size), grads_t)
     set_terms(slice(0, size), grads_t * (-1.0 / examples))
 
+    for k, here in enumerate(stripes):
+        copies[k].wait()
+        stop = (k + 1) * B
+        spot = slice(k * B, stop)
+        work[here, 0 : here.stop] = held[here, 0 : here.stop].astype(jnp.float32)
+        if here.stop < stop:
+            work[here.stop : stop, 0:stop] = jnp.zeros((stop - size, stop), jnp.float32)
+            work[here, here.stop : stop] = jnp.zeros((size - k * B, stop - size), jnp.float32)
+        work[spot, spot] += jnp.where(r == c, jnp.where(r + k * B < size, damp_ref[0], 1.0), 0.0)
+
     def product(x, y):
         return lax.dot_general(x, y, (((1,), (1,)), ((), ())), preferred_element_type=jnp.float32)
 
@@ -165,7 +175,8 @@
 
 
 def scores_of(prior, damping, first, slots, queries, own):
-    blocks = pl.cdiv(prior.shape[0], B)
+    size = prior.shape[0]
+    blocks = pl.cdiv(size, B)
     most = max(b - a for a, b in zip(STARTS, (*STARTS[1:], blocks - 1)))
     width = (blocks + most) * B
     vmem = pl.BlockSpec(memory_space=pltpu.VMEM)
@@ -173,14 +184,16 @@
     return pl.pallas_call(
         solve_kernel,
         out_shape=jax.ShapeDtypeStruct((own, queries.shape[0]), jnp.float32),
-        in_specs=[vmem, smem, smem, vmem, vmem],
+        in_specs=[pl.BlockSpec(memory_space=pl.ANY), smem, smem, vmem, vmem],
         out_specs=vmem,
         scratch_shapes=[
+            pltpu.VMEM((size, size), prior.dtype),
             pltpu.VMEM((width, width), jnp.float32),
             pltpu.VMEM((width, 3 * B), jnp.bfloat16),
             pltpu.VMEM((width, 3 * B), jnp.bfloat16),
+            pltpu.SemaphoreType.DMA((blocks,)),
         ],
-        compiler_params=pltpu.CompilerParams(vmem_limit_bytes=36 * 2**20),
+        compiler_params=pltpu.CompilerParams(vmem_limit_bytes=60 * 2**20),
     )(prior, damping, first, slots, queries)
 
 

time: 107 us -> 109 us (1.019)
  Pallas kernels: 48.7 us -> 51.6 us
  local copies, waits for them, and re-layouts: 4.39 us -> 2.8 us
    pallas_call x1, Pallas kernels: 48.7 us -> 51.6 us  [scores_of(): pl.pallas_call(solve_kernel, out_shape=jax.ShapeDtypeStruct((own, queries...]
    unnamed x13 -> x9, local copies, waits for them, and re-layouts: 3.8 us -> 1.29 us
where the time goes in v4:
time: 109 us
  Pallas kernels  51.6 us (47%)
  blocking collectives  17.3 us (16%)
  matrix products  13.4 us (12%)
  waiting for transfers between devices  11.2 us (10%)
  starting transfers between devices  10.2 us (9%)
  local copies, waits for them, and re-layouts  2.8 us (3%)
  other arithmetic  1.84 us (2%)
    pallas_call x1, Pallas kernels, scores_of(): pl.pallas_call(solve_kernel, out_shape=jax.ShapeDtypeStruct((own, queries...  51.6 us
    all_to_all x1, blocking collectives, gather_pairs(): lax.all_to_all(spread, axis, 0, 0, axis_index_groups=groups, tiled=True)  17.3 us
    dot_general x1, matrix products, per_device(): jnp.einsum('ltf,lkf->ltk', activations, proj_in, preferred_element_type=j...  9.55 us
    ppermute x3, waiting for transfers between devices, to_layer(): lax.ppermute(piece, axis, [(i, (i + d) % length) for i in range(length)])  6.5 us
    ppermute x3, starting transfers between devices, to_layer(): lax.ppermute(piece, axis, [(i, (i + d) % length) for i in range(length)])  5.4 us
    ppermute x3, starting transfers between devices, sum_of_four(): lax.ppermute(x, axis, [(i, i ^ d) for i in range(4)])  4.78 us
    ppermute x3, waiting for transfers between devices, sum_of_four(): lax.ppermute(x, axis, [(i, i ^ d) for i in range(4)])  3.62 us
    dot_general x1, matrix products, per_device(): jnp.einsum('ltf,lkf->ltk', out_grads, proj_out, preferred_element_type=jn...  3.55 us
  transfers between devices with their start and end apart: 7, of which 6 were waited for; matrix products, arithmetic and copies ran while one was open for 0% of the time, Pallas kernels for 0%

profile of v4, /device:TPU:0, one launch (start us, length us, event | category | flops | bytes accessed | tf_op | source)
XLA Modules:
  0.0 109.1 jit_solution(7102573666242101686)
XLA Ops:
  0.0 0.0 copy-start
  0.0 1.3 %copy-done = bf16[4,40,3584]{2,1,0:T(8,128)(2,1)S(1)} copy-done((bf16[4,40,3584]{2,1,0:T(8,128)(2,1)S(1)}, bf16[4,40,3584]{2,1,0:T(8,128)(2,1)}, u32[]{:S(2)}) %copy-start) | copy-done | bytes 1146904
  1.3 0.0 copy-start.1
  1.3 9.6 %fusion.17 = f32[4,512,40]{1,2,0:T(8,128)S(1)} fusion(bf16[4,512,3584]{2,1,0:T(8,128)(2,1)} %param.9, bf16[4,40,3584]{2,1,0:T(8,128)(2,1)S(1)} %copy-done), kind=kOutput, calls=%fused_computation.34 | convolution fusion | flops 587202560 | bytes 16154624 | tf_op jit(solution)/shard_map/ltf,lkf->ltk/dot_general | solution.py:237
  10.8 0.0 copy-done.1
  10.8 0.0 copy-start.3
  10.9 0.0 copy-start.2
  10.9 3.6 %fusion.18 = f32[4,512,40]{1,2,0:T(8,128)S(1)} fusion(bf16[4,512,1024]{2,1,0:T(8,128)(2,1)} %param.10, bf16[4,40,1024]{2,1,0:T(8,128)(2,1)S(1)} %copy-done.1), kind=kOutput, calls=%fused_computation.35 | convolution fusion | flops 167772160 | bytes 4849664 | tf_op jit(solution)/shard_map/ltf,lkf->ltk/dot_general | solution.py:238
  14.5 1.8 %collective-permute-start = (f32[1024,40]{0,1:T(8,128)S(1)}, f32[1024,40]{0,1:T(8,128)S(1)}, u32[]{:S(2)}, u32[]{:S(2)}) collective-permute-start(f32[1024,40]{0,1:T(8,128)S(1)} %get-tuple-element.7), channel_id=1, source_target_pairs={{0,1},{1,2},{2,3},{3,0},{4,5},{5,6},{6,7},{7,4},{8,9},{9,10},{10,1... | collective-permute-start | bytes 491528 | tf_op jit(solution)/shard_map/ppermute | solution.py:206
  16.2 1.5 %collective-permute-start.1 = (f32[1024,40]{0,1:T(8,128)S(1)}, f32[1024,40]{0,1:T(8,128)S(1)}, u32[]{:S(2)}, u32[]{:S(2)}) collective-permute-start(f32[1024,40]{0,1:T(8,128)S(1)} %get-tuple-element.8), channel_id=1, source_target_pairs={{0,3},{1,0},{2,1},{3,2},{4,7},{5,4},{6,5},{7,6},{8,11},{9,8},{10,9... | collective-permute-start | bytes 491528 | tf_op jit(solution)/shard_map/ppermute | solution.py:206
  17.8 2.1 %collective-permute-start.2 = (f32[1024,40]{0,1:T(8,128)S(1)}, f32[1024,40]{0,1:T(8,128)S(1)}, u32[]{:S(2)}, u32[]{:S(2)}) collective-permute-start(f32[1024,40]{0,1:T(8,128)S(1)} %get-tuple-element.9), channel_id=1, source_target_pairs={{0,2},{1,3},{2,0},{3,1},{4,6},{5,7},{6,4},{7,5},{8,10},{9,11},{10,... | collective-permute-start | bytes 491528 | tf_op jit(solution)/shard_map/ppermute | solution.py:206
  19.9 0.0 copy-done.3
  19.9 0.1 copy.14
  20.0 0.0 copy-done.2
  20.0 0.1 fusion.15
  20.1 1.8 %collective-permute-done = f32[1024,40]{0,1:T(8,128)S(1)} collective-permute-done((f32[1024,40]{0,1:T(8,128)S(1)}, f32[1024,40]{0,1:T(8,128)S(1)}, u32[]{:S(2)}, u32[]{:S(2)}) %collective-permute-start) | collective-permute-done | bytes 163872 | tf_op jit(solution)/shard_map/ppermute | solution.py:206
  21.9 2.9 %collective-permute-done.1 = f32[1024,40]{0,1:T(8,128)S(1)} collective-permute-done((f32[1024,40]{0,1:T(8,128)S(1)}, f32[1024,40]{0,1:T(8,128)S(1)}, u32[]{:S(2)}, u32[]{:S(2)}) %collective-permute-start.1) | collective-permute-done | bytes 163872 | tf_op jit(solution)/shard_map/ppermute | solution.py:206
  24.8 1.8 %collective-permute-done.2 = f32[1024,40]{0,1:T(8,128)S(1)} collective-permute-done((f32[1024,40]{0,1:T(8,128)S(1)}, f32[1024,40]{0,1:T(8,128)S(1)}, u32[]{:S(2)}, u32[]{:S(2)}) %collective-permute-start.2) | collective-permute-done | bytes 163872 | tf_op jit(solution)/shard_map/ppermute | solution.py:206
  26.7 0.3 fusion.11
  27.0 0.1 reshape.37
  27.1 0.1 pad_maximum_fusion.1
  27.2 0.1 broadcast_in_dim.8
  27.2 17.3 %all_to_all.5 = f32[16,4,1601]{2,1,0:T(4,128)S(1)} all-to-all(f32[16,4,1601]{2,1,0:T(4,128)S(1)} %broadcast_in_dim.8), channel_id=1, replica_groups={{0,8,16,24,32,40,48,56,64,72,80,88,96,104,112,120},{4,12,20,28,36,44,52..., dimensions={0} | all-to-all | bytes 819712 | tf_op jit(solution)/shard_map/all_to_all | solution.py:215
  44.5 0.0 collective-permute-start.3
  45.1 1.1 %collective-permute-done.3 = f32[16,4,1601]{2,1,0:T(4,128)S(1)} collective-permute-done((f32[16,4,1601]{2,1,0:T(4,128)S(1)}, f32[16,4,1601]{2,1,0:T(4,128)S(1)}, u32[]{:S(2)}, u32[]{:S(2)}) %collective-permute-start.3) | collective-permute-done | bytes 409888 | tf_op jit(solution)/shard_map/ppermute | solution.py:216
  46.2 0.1 select_bitcast_fusion.1
  46.4 0.2 pad_maximum_fusion
  46.6 1.2 %reshape.38.slots_ref = f32[128,1601]{1,0:T(8,128)} reshape(f32[16,2,4,1601]{3,2,1,0:T(4,128)S(1)} %pad_maximum_fusion) | data formatting | bytes 1639424 | tf_op jit(solution)/shard_map/reshape | solution.py:219
  47.8 51.6 %shard_map.91 = f32[4,64]{1,0:T(4,128)} custom-call(bf16[1600,1600]{1,0:T(8,128)(2,1)} %bitcast.39, f32[1]{0:T(128)S(6)} %copy.23.damp_ref, s32[1]{0:T(128)} %bitcast.1.first_ref, f32[128,1601]{1,0:T(8,128)} %reshape.38.slots_ref, f32[64,1600]{1,0:T(8,128)} %bitcast.40), custom_call_target="tpu_custom_call" | custom-call | tf_op jit(solution)/shard_map/pallas_call | solution.py:184
  99.4 1.2 %collective-permute-start.4 = (f32[4,64]{1,0:T(4,128)}, f32[4,64]{1,0:T(4,128)S(1)}, u32[]{:S(2)}, u32[]{:S(2)}) collective-permute-start(f32[4,64]{1,0:T(4,128)} %shard_map.91), channel_id=1, source_target_pairs={{0,1},{1,0},{2,3},{3,2},{4,5},{5,4},{6,7},{7,6},{8,9},{9,8},{10,11... | collective-permute-start | bytes 3080 | tf_op jit(solution)/shard_map/ppermute | solution.py:223
  100.6 2.2 %collective-permute-start.5 = (f32[4,64]{1,0:T(4,128)}, f32[4,64]{1,0:T(4,128)S(1)}, u32[]{:S(2)}, u32[]{:S(2)}) collective-permute-start(f32[4,64]{1,0:T(4,128)} %shard_map.91), channel_id=1, source_target_pairs={{0,2},{1,3},{2,0},{3,1},{4,6},{5,7},{6,4},{7,5},{8,10},{9,11},{10,... | collective-permute-start | bytes 3080 | tf_op jit(solution)/shard_map/ppermute | solution.py:223
  102.8 1.4 %collective-permute-start.6 = (f32[4,64]{1,0:T(4,128)}, f32[4,64]{1,0:T(4,128)S(1)}, u32[]{:S(2)}, u32[]{:S(2)}) collective-permute-start(f32[4,64]{1,0:T(4,128)} %shard_map.91), channel_id=1, source_target_pairs={{0,3},{1,2},{2,1},{3,0},{4,7},{5,6},{6,5},{7,4},{8,11},{9,10},{10,... | collective-permute-start | bytes 3080 | tf_op jit(solution)/shard_map/ppermute | solution.py:223
  104.2 0.0 collective-permute-done.4
  104.2 1.7 %collective-permute-done.5 = f32[4,64]{1,0:T(4,128)S(1)} collective-permute-done((f32[4,64]{1,0:T(4,128)}, f32[4,64]{1,0:T(4,128)S(1)}, u32[]{:S(2)}, u32[]{:S(2)}) %collective-permute-start.5) | collective-permute-done | bytes 1056 | tf_op jit(solution)/shard_map/ppermute | solution.py:223
  105.9 1.9 %collective-permute-done.6 = f32[4,64]{1,0:T(4,128)S(1)} collective-permute-done((f32[4,64]{1,0:T(4,128)}, f32[4,64]{1,0:T(4,128)S(1)}, u32[]{:S(2)}, u32[]{:S(2)}) %collective-permute-start.6) | collective-permute-done | bytes 1056 | tf_op jit(solution)/shard_map/ppermute | solution.py:223
  107.8 1.3 %add_add_fusion = f32[4,64]{1,0:T(4,128)} fusion(f32[4,64]{1,0:T(4,128)S(1)} %collective-permute-done.5, f32[4,64]{1,0:T(4,128)S(1)} %collective-permute-done.6, f32[4,64]{1,0:T(4,128)} %shard_map.91, f32[4,64]{1,0:T(4,128)S(1)} %collective-permute-done.4), kind=kLoop, calls=%fused_computation.29 | loop fusion | flops 768 | bytes 5120 | tf_op jit(solution)/shard_map/add | solution.py:224
  (7 shorter events, 0.1 us)
Async XLA Ops:
  0.0 1.3 %copy-start = (bf16[4,40,3584]{2,1,0:T(8,128)(2,1)S(1)}, bf16[4,40,3584]{2,1,0:T(8,128)(2,1)}, u32[]{:S(2)}) copy-start(bf16[4,40,3584]{2,1,0:T(8,128)(2,1)} %param.11) | copy-start | bytes 3440644
  1.3 9.6 %copy-start.1 = (bf16[4,40,1024]{2,1,0:T(8,128)(2,1)S(1)}, bf16[4,40,1024]{2,1,0:T(8,128)(2,1)}, u32[]{:S(2)}) copy-start(bf16[4,40,1024]{2,1,0:T(8,128)(2,1)} %param.12) | copy-start | bytes 983044
  10.8 9.0 %copy-start.3 = (s32[4]{0:T(128)S(1)}, s32[4]{0:T(128)}, u32[]{:S(2)}) copy-start(s32[4]{0:T(128)} %param.14) | copy-start | bytes 52
  10.9 9.1 %copy-start.2 = (s32[4]{0:T(128)S(1)}, s32[4]{0:T(128)}, u32[]{:S(2)}) copy-start(s32[4]{0:T(128)} %param.13) | copy-start | bytes 52
  14.5 7.4 %collective-permute-start = (f32[1024,40]{0,1:T(8,128)S(1)}, f32[1024,40]{0,1:T(8,128)S(1)}, u32[]{:S(2)}, u32[]{:S(2)}) collective-permute-start(f32[1024,40]{0,1:T(8,128)S(1)} %get-tuple-element.7), channel_id=1, source_target_pairs={{0,1},{1,2},{2,3},{3,0},{4,5},{5,6},{6,7},{7,4},{8,9},{9,10},{10,1... | collective-permute-start | bytes 491528 | tf_op jit(solution)/shard_map/ppermute | solution.py:206
  16.2 8.5 %collective-permute-start.1 = (f32[1024,40]{0,1:T(8,128)S(1)}, f32[1024,40]{0,1:T(8,128)S(1)}, u32[]{:S(2)}, u32[]{:S(2)}) collective-permute-start(f32[1024,40]{0,1:T(8,128)S(1)} %get-tuple-element.8), channel_id=1, source_target_pairs={{0,3},{1,0},{2,1},{3,2},{4,7},{5,4},{6,5},{7,6},{8,11},{9,8},{10,9... | collective-permute-start | bytes 491528 | tf_op jit(solution)/shard_map/ppermute | solution.py:206
  17.8 8.8 %collective-permute-start.2 = (f32[1024,40]{0,1:T(8,128)S(1)}, f32[1024,40]{0,1:T(8,128)S(1)}, u32[]{:S(2)}, u32[]{:S(2)}) collective-permute-start(f32[1024,40]{0,1:T(8,128)S(1)} %get-tuple-element.9), channel_id=1, source_target_pairs={{0,2},{1,3},{2,0},{3,1},{4,6},{5,7},{6,4},{7,5},{8,10},{9,11},{10,... | collective-permute-start | bytes 491528 | tf_op jit(solution)/shard_map/ppermute | solution.py:206
  44.5 1.8 %collective-permute-start.3 = (f32[16,4,1601]{2,1,0:T(4,128)S(1)}, f32[16,4,1601]{2,1,0:T(4,128)S(1)}, u32[]{:S(2)}, u32[]{:S(2)}) collective-permute-start(f32[16,4,1601]{2,1,0:T(4,128)S(1)} %all_to_all.5), channel_id=1, source_target_pairs={{0,4},{4,0},{8,12},{12,8},{16,20},{20,16},{24,28},{28,24},{32,36},... | collective-permute-start | bytes 1229576 | tf_op jit(solution)/shard_map/ppermute | solution.py:216
  99.4 4.8 %collective-permute-start.4 = (f32[4,64]{1,0:T(4,128)}, f32[4,64]{1,0:T(4,128)S(1)}, u32[]{:S(2)}, u32[]{:S(2)}) collective-permute-start(f32[4,64]{1,0:T(4,128)} %shard_map.91), channel_id=1, source_target_pairs={{0,1},{1,0},{2,3},{3,2},{4,5},{5,4},{6,7},{7,6},{8,9},{9,8},{10,11... | collective-permute-start | bytes 3080 | tf_op jit(solution)/shard_map/ppermute | solution.py:223
  100.6 5.3 %collective-permute-start.5 = (f32[4,64]{1,0:T(4,128)}, f32[4,64]{1,0:T(4,128)S(1)}, u32[]{:S(2)}, u32[]{:S(2)}) collective-permute-start(f32[4,64]{1,0:T(4,128)} %shard_map.91), channel_id=1, source_target_pairs={{0,2},{1,3},{2,0},{3,1},{4,6},{5,7},{6,4},{7,5},{8,10},{9,11},{10,... | collective-permute-start | bytes 3080 | tf_op jit(solution)/shard_map/ppermute | solution.py:223
  102.8 5.0 %collective-permute-start.6 = (f32[4,64]{1,0:T(4,128)}, f32[4,64]{1,0:T(4,128)S(1)}, u32[]{:S(2)}, u32[]{:S(2)}) collective-permute-start(f32[4,64]{1,0:T(4,128)} %shard_map.91), channel_id=1, source_target_pairs={{0,3},{1,2},{2,1},{3,0},{4,7},{5,6},{6,5},{7,4},{8,11},{9,10},{10,... | collective-permute-start | bytes 3080 | tf_op jit(solution)/shard_map/ppermute | solution.py:223

commit v5 on v3

--- a/solution.py
+++ b/solution.py
@@ -8,7 +8,7 @@
 KP = 40
 B = 128
 S = 16
-STARTS = (0, 3, 6, 9)
+STARTS = (0, 2, 4, 6, 8, 10)
 
 
 def split(x):
@@ -85,7 +85,6 @@
     examples = slots_ref.shape[0]
     n_query = queries_ref.shape[0]
     n_own = out_ref.shape[0]
-    whole = size // B * B
     r = lax.broadcasted_iota(jnp.int32, (B, B), 0)
     c = lax.broadcasted_iota(jnp.int32, (B, B), 1)
 
@@ -221,8 +220,9 @@
     live_mask = (jnp.arange(seq_len, dtype=jnp.int32)[None, :] < lengths[:, None]).astype(
         jnp.float32
     )
+    out_parts = jnp.einsum("ltf,lkf->ltk", out_grads, proj_out, preferred_element_type=jnp.float32)
+    activations, out_parts = lax.optimization_barrier((activations, out_parts))
     in_parts = jnp.einsum("ltf,lkf->ltk", activations, proj_in, preferred_element_type=jnp.float32)
-    out_parts = jnp.einsum("ltf,lkf->ltk", out_grads, proj_out, preferred_element_type=jnp.float32)
     owned = to_layer(jnp.concatenate([in_parts, out_parts], axis=1), "tensor")
     in_rows = owned[:tokens].reshape(ex_local, seq_len, KP) * live_mask[:, :, None]
     out_rows = owned[tokens:].reshape(ex_local, seq_len, KP)

time: 107 us -> 105 us (0.981)
  local copies, waits for them, and re-layouts: 4.39 us -> 3.12 us
    unnamed x13 -> x11, local copies, waits for them, and re-layouts: 3.8 us -> 2.53 us
where the time goes in v5:
time: 105 us
  Pallas kernels  47.7 us (45%)
  blocking collectives  17.3 us (16%)
  matrix products  13.5 us (13%)
  waiting for transfers between devices  11 us (10%)
  starting transfers between devices  10.2 us (10%)
  local copies, waits for them, and re-layouts  3.12 us (3%)
  other arithmetic  1.17 us (1%)
    pallas_call x1, Pallas kernels, scores_of(): pl.pallas_call(solve_kernel, out_shape=jax.ShapeDtypeStruct((own, queries...  47.7 us
    all_to_all x1, blocking collectives, gather_pairs(): lax.all_to_all(spread, axis, 0, 0, axis_index_groups=groups, tiled=True)  17.3 us
    dot_general x1, matrix products, per_device(): jnp.einsum('ltf,lkf->ltk', activations, proj_in, preferred_element_type=j...  9.52 us
    ppermute x3, waiting for transfers between devices, to_layer(): lax.ppermute(piece, axis, [(i, (i + d) % length) for i in range(length)])  6.5 us
    ppermute x3, starting transfers between devices, to_layer(): lax.ppermute(piece, axis, [(i, (i + d) % length) for i in range(length)])  5.4 us
    ppermute x3, starting transfers between devices, sum_of_four(): lax.ppermute(x, axis, [(i, i ^ d) for i in range(4)])  4.78 us
    dot_general x1, matrix products, per_device(): jnp.einsum('ltf,lkf->ltk', out_grads, proj_out, preferred_element_type=jn...  3.69 us
    ppermute x3, waiting for transfers between devices, sum_of_four(): lax.ppermute(x, axis, [(i, i ^ d) for i in range(4)])  3.4 us
  transfers between devices with their start and end apart: 7, of which 6 were waited for; matrix products, arithmetic and copies ran while one was open for 0% of the time, Pallas kernels for 0%

profile of v5, /device:TPU:0, one launch (start us, length us, event | category | flops | bytes accessed | tf_op | source)
XLA Modules:
  0.0 104.7 jit_solution(13554416364348816365)
XLA Ops:
  0.0 0.0 copy-start
  0.0 3.7 %fusion.17 = f32[4,512,40]{1,2,0:T(8,128)S(1)} fusion(bf16[4,512,1024]{2,1,0:T(8,128)(2,1)} %param.10, bf16[4,40,1024]{2,1,0:T(8,128)(2,1)} %param.12), kind=kOutput, calls=%fused_computation.34 | convolution fusion | flops 167772160 | bytes 4849664 | tf_op jit(solution)/shard_map/ltf,lkf->ltk/dot_general | solution.py:223
  3.7 0.0 copy-done
  3.7 0.0 copy-start.4
  3.7 0.0 copy-start.3
  3.7 9.5 %fusion.18 = f32[4,512,40]{1,2,0:T(8,128)S(1)} fusion(bf16[4,512,3584]{2,1,0:T(8,128)(2,1)} %param.9, bf16[4,40,3584]{2,1,0:T(8,128)(2,1)S(1)} %copy-done), kind=kOutput, calls=%fused_computation.35 | convolution fusion | flops 587202560 | bytes 16154624 | tf_op jit(solution)/shard_map/ltf,lkf->ltk/dot_general | solution.py:225
  13.3 0.1 fusion.8
  13.3 1.8 %collective-permute-start = (f32[1024,40]{0,1:T(8,128)S(1)}, f32[1024,40]{0,1:T(8,128)S(1)}, u32[]{:S(2)}, u32[]{:S(2)}) collective-permute-start(f32[1024,40]{0,1:T(8,128)S(1)} %get-tuple-element.11), channel_id=1, source_target_pairs={{0,1},{1,2},{2,3},{3,0},{4,5},{5,6},{6,7},{7,4},{8,9},{9,10},{10,1... | collective-permute-start | bytes 491528 | tf_op jit(solution)/shard_map/ppermute | solution.py:192
  15.1 1.5 %collective-permute-start.1 = (f32[1024,40]{0,1:T(8,128)S(1)}, f32[1024,40]{0,1:T(8,128)S(1)}, u32[]{:S(2)}, u32[]{:S(2)}) collective-permute-start(f32[1024,40]{0,1:T(8,128)S(1)} %get-tuple-element.12), channel_id=1, source_target_pairs={{0,3},{1,0},{2,1},{3,2},{4,7},{5,4},{6,5},{7,6},{8,11},{9,8},{10,9... | collective-permute-start | bytes 491528 | tf_op jit(solution)/shard_map/ppermute | solution.py:192
  16.6 2.1 %collective-permute-start.2 = (f32[1024,40]{0,1:T(8,128)S(1)}, f32[1024,40]{0,1:T(8,128)S(1)}, u32[]{:S(2)}, u32[]{:S(2)}) collective-permute-start(f32[1024,40]{0,1:T(8,128)S(1)} %get-tuple-element.13), channel_id=1, source_target_pairs={{0,2},{1,3},{2,0},{3,1},{4,6},{5,7},{6,4},{7,5},{8,10},{9,11},{10,... | collective-permute-start | bytes 491528 | tf_op jit(solution)/shard_map/ppermute | solution.py:192
  18.7 0.0 copy-done.4
  18.7 0.1 copy.14
  18.8 0.0 copy-done.3
  18.8 0.1 fusion.15
  18.9 0.0 copy-start.2
  18.9 1.8 %collective-permute-done = f32[1024,40]{0,1:T(8,128)S(1)} collective-permute-done((f32[1024,40]{0,1:T(8,128)S(1)}, f32[1024,40]{0,1:T(8,128)S(1)}, u32[]{:S(2)}, u32[]{:S(2)}) %collective-permute-start) | collective-permute-done | bytes 163872 | tf_op jit(solution)/shard_map/ppermute | solution.py:192
  20.7 2.9 %collective-permute-done.1 = f32[1024,40]{0,1:T(8,128)S(1)} collective-permute-done((f32[1024,40]{0,1:T(8,128)S(1)}, f32[1024,40]{0,1:T(8,128)S(1)}, u32[]{:S(2)}, u32[]{:S(2)}) %collective-permute-start.1) | collective-permute-done | bytes 163872 | tf_op jit(solution)/shard_map/ppermute | solution.py:192
  23.6 1.8 %collective-permute-done.2 = f32[1024,40]{0,1:T(8,128)S(1)} collective-permute-done((f32[1024,40]{0,1:T(8,128)S(1)}, f32[1024,40]{0,1:T(8,128)S(1)}, u32[]{:S(2)}, u32[]{:S(2)}) %collective-permute-start.2) | collective-permute-done | bytes 163872 | tf_op jit(solution)/shard_map/ppermute | solution.py:192
  25.5 0.3 fusion.11
  25.8 0.1 reshape.37
  25.9 0.1 pad_maximum_fusion.1
  26.0 0.1 broadcast_in_dim.8
  26.1 17.3 %all_to_all.5 = f32[16,4,1601]{2,1,0:T(4,128)S(1)} all-to-all(f32[16,4,1601]{2,1,0:T(4,128)S(1)} %broadcast_in_dim.8), channel_id=1, replica_groups={{0,8,16,24,32,40,48,56,64,72,80,88,96,104,112,120},{4,12,20,28,36,44,52..., dimensions={0} | all-to-all | bytes 819712 | tf_op jit(solution)/shard_map/all_to_all | solution.py:201
  43.3 0.0 collective-permute-start.3
  44.0 1.1 %collective-permute-done.3 = f32[16,4,1601]{2,1,0:T(4,128)S(1)} collective-permute-done((f32[16,4,1601]{2,1,0:T(4,128)S(1)}, f32[16,4,1601]{2,1,0:T(4,128)S(1)}, u32[]{:S(2)}, u32[]{:S(2)}) %collective-permute-start.3) | collective-permute-done | bytes 409888 | tf_op jit(solution)/shard_map/ppermute | solution.py:202
  45.1 0.1 select_bitcast_fusion.1
  45.2 0.2 pad_maximum_fusion
  45.4 0.3 reshape.38.slots_ref
  45.7 0.0 copy-done.2
  45.8 0.0 copy-start.1
  45.8 2.5 %copy-done.1 = bf16[1,1600,1600]{2,1,0:T(8,128)(2,1)S(1)} copy-done((bf16[1,1600,1600]{2,1,0:T(8,128)(2,1)S(1)}, bf16[1,1600,1600]{2,1,0:T(8,128)(2,1)}, u32[]{:S(2)}) %copy-start.1) | copy-done | bytes 5120024
  48.3 47.7 %shard_map.91 = f32[4,64]{1,0:T(4,128)S(1)} custom-call(bf16[1600,1600]{1,0:T(8,128)(2,1)S(1)} %bitcast.39, f32[1]{0:T(128)S(6)} %copy.23.damp_ref, s32[1]{0:T(128)} %bitcast.1.first_ref, f32[128,1601]{1,0:T(8,128)S(1)} %reshape.38.slots_ref, f32[64,1600]{1,0:T(8,128)S(1)} %bitcast.40), custom_call_target="tpu_custom_call" | custom-call | tf_op jit(solution)/shard_map/pallas_call | solution.py:172
  96.0 1.2 %collective-permute-start.4 = (f32[4,64]{1,0:T(4,128)S(1)}, f32[4,64]{1,0:T(4,128)S(1)}, u32[]{:S(2)}, u32[]{:S(2)}) collective-permute-start(f32[4,64]{1,0:T(4,128)S(1)} %shard_map.91), channel_id=1, source_target_pairs={{0,1},{1,0},{2,3},{3,2},{4,5},{5,4},{6,7},{7,6},{8,9},{9,8},{10,11... | collective-permute-start | bytes 3080 | tf_op jit(solution)/shard_map/ppermute | solution.py:209
  97.2 2.2 %collective-permute-start.5 = (f32[4,64]{1,0:T(4,128)S(1)}, f32[4,64]{1,0:T(4,128)S(1)}, u32[]{:S(2)}, u32[]{:S(2)}) collective-permute-start(f32[4,64]{1,0:T(4,128)S(1)} %shard_map.91), channel_id=1, source_target_pairs={{0,2},{1,3},{2,0},{3,1},{4,6},{5,7},{6,4},{7,5},{8,10},{9,11},{10,... | collective-permute-start | bytes 3080 | tf_op jit(solution)/shard_map/ppermute | solution.py:209
  99.4 1.4 %collective-permute-start.6 = (f32[4,64]{1,0:T(4,128)S(1)}, f32[4,64]{1,0:T(4,128)S(1)}, u32[]{:S(2)}, u32[]{:S(2)}) collective-permute-start(f32[4,64]{1,0:T(4,128)S(1)} %shard_map.91), channel_id=1, source_target_pairs={{0,3},{1,2},{2,1},{3,0},{4,7},{5,6},{6,5},{7,4},{8,11},{9,10},{10,... | collective-permute-start | bytes 3080 | tf_op jit(solution)/shard_map/ppermute | solution.py:209
  100.8 0.0 collective-permute-done.4
  100.8 1.5 %collective-permute-done.5 = f32[4,64]{1,0:T(4,128)S(1)} collective-permute-done((f32[4,64]{1,0:T(4,128)S(1)}, f32[4,64]{1,0:T(4,128)S(1)}, u32[]{:S(2)}, u32[]{:S(2)}) %collective-permute-start.5) | collective-permute-done | bytes 1056 | tf_op jit(solution)/shard_map/ppermute | solution.py:209
  102.3 1.9 %collective-permute-done.6 = f32[4,64]{1,0:T(4,128)S(1)} collective-permute-done((f32[4,64]{1,0:T(4,128)S(1)}, f32[4,64]{1,0:T(4,128)S(1)}, u32[]{:S(2)}, u32[]{:S(2)}) %collective-permute-start.6) | collective-permute-done | bytes 1056 | tf_op jit(solution)/shard_map/ppermute | solution.py:209
  104.2 0.6 add_add_fusion
  (6 shorter events, 0.1 us)
Async XLA Ops:
  0.0 3.7 %copy-start = (bf16[4,40,3584]{2,1,0:T(8,128)(2,1)S(1)}, bf16[4,40,3584]{2,1,0:T(8,128)(2,1)}, u32[]{:S(2)}) copy-start(bf16[4,40,3584]{2,1,0:T(8,128)(2,1)} %param.11) | copy-start | bytes 3440644
  3.7 15.0 %copy-start.4 = (s32[4]{0:T(128)S(1)}, s32[4]{0:T(128)}, u32[]{:S(2)}) copy-start(s32[4]{0:T(128)} %param.14) | copy-start | bytes 52
  3.7 15.1 %copy-start.3 = (s32[4]{0:T(128)S(1)}, s32[4]{0:T(128)}, u32[]{:S(2)}) copy-start(s32[4]{0:T(128)} %param.13) | copy-start | bytes 52
  13.3 7.4 %collective-permute-start = (f32[1024,40]{0,1:T(8,128)S(1)}, f32[1024,40]{0,1:T(8,128)S(1)}, u32[]{:S(2)}, u32[]{:S(2)}) collective-permute-start(f32[1024,40]{0,1:T(8,128)S(1)} %get-tuple-element.11), channel_id=1, source_target_pairs={{0,1},{1,2},{2,3},{3,0},{4,5},{5,6},{6,7},{7,4},{8,9},{9,10},{10,1... | collective-permute-start | bytes 491528 | tf_op jit(solution)/shard_map/ppermute | solution.py:192
  15.1 8.5 %collective-permute-start.1 = (f32[1024,40]{0,1:T(8,128)S(1)}, f32[1024,40]{0,1:T(8,128)S(1)}, u32[]{:S(2)}, u32[]{:S(2)}) collective-permute-start(f32[1024,40]{0,1:T(8,128)S(1)} %get-tuple-element.12), channel_id=1, source_target_pairs={{0,3},{1,0},{2,1},{3,2},{4,7},{5,4},{6,5},{7,6},{8,11},{9,8},{10,9... | collective-permute-start | bytes 491528 | tf_op jit(solution)/shard_map/ppermute | solution.py:192
  16.6 8.8 %collective-permute-start.2 = (f32[1024,40]{0,1:T(8,128)S(1)}, f32[1024,40]{0,1:T(8,128)S(1)}, u32[]{:S(2)}, u32[]{:S(2)}) collective-permute-start(f32[1024,40]{0,1:T(8,128)S(1)} %get-tuple-element.13), channel_id=1, source_target_pairs={{0,2},{1,3},{2,0},{3,1},{4,6},{5,7},{6,4},{7,5},{8,10},{9,11},{10,... | collective-permute-start | bytes 491528 | tf_op jit(solution)/shard_map/ppermute | solution.py:192
  18.9 26.8 %copy-start.2 = (f32[1,64,1600]{2,1,0:T(8,128)S(1)}, f32[1,64,1600]{2,1,0:T(8,128)}, u32[]{:S(2)}) copy-start(f32[1,64,1600]{2,1,0:T(8,128)} %param.17) | copy-start | bytes 1228804
  43.3 1.8 %collective-permute-start.3 = (f32[16,4,1601]{2,1,0:T(4,128)S(1)}, f32[16,4,1601]{2,1,0:T(4,128)S(1)}, u32[]{:S(2)}, u32[]{:S(2)}) collective-permute-start(f32[16,4,1601]{2,1,0:T(4,128)S(1)} %all_to_all.5), channel_id=1, source_target_pairs={{0,4},{4,0},{8,12},{12,8},{16,20},{20,16},{24,28},{28,24},{32,36},... | collective-permute-start | bytes 1229576 | tf_op jit(solution)/shard_map/ppermute | solution.py:202
  45.8 2.5 %copy-start.1 = (bf16[1,1600,1600]{2,1,0:T(8,128)(2,1)S(1)}, bf16[1,1600,1600]{2,1,0:T(8,128)(2,1)}, u32[]{:S(2)}) copy-start(bf16[1,1600,1600]{2,1,0:T(8,128)(2,1)} %param.15) | copy-start | bytes 15360004
  96.0 4.8 %collective-permute-start.4 = (f32[4,64]{1,0:T(4,128)S(1)}, f32[4,64]{1,0:T(4,128)S(1)}, u32[]{:S(2)}, u32[]{:S(2)}) collective-permute-start(f32[4,64]{1,0:T(4,128)S(1)} %shard_map.91), channel_id=1, source_target_pairs={{0,1},{1,0},{2,3},{3,2},{4,5},{5,4},{6,7},{7,6},{8,9},{9,8},{10,11... | collective-permute-start | bytes 3080 | tf_op jit(solution)/shard_map/ppermute | solution.py:209
  97.2 5.1 %collective-permute-start.5 = (f32[4,64]{1,0:T(4,128)S(1)}, f32[4,64]{1,0:T(4,128)S(1)}, u32[]{:S(2)}, u32[]{:S(2)}) collective-permute-start(f32[4,64]{1,0:T(4,128)S(1)} %shard_map.91), channel_id=1, source_target_pairs={{0,2},{1,3},{2,0},{3,1},{4,6},{5,7},{6,4},{7,5},{8,10},{9,11},{10,... | collective-permute-start | bytes 3080 | tf_op jit(solution)/shard_map/ppermute | solution.py:209
  99.4 4.8 %collective-permute-start.6 = (f32[4,64]{1,0:T(4,128)S(1)}, f32[4,64]{1,0:T(4,128)S(1)}, u32[]{:S(2)}, u32[]{:S(2)}) collective-permute-start(f32[4,64]{1,0:T(4,128)S(1)} %shard_map.91), channel_id=1, source_target_pairs={{0,3},{1,2},{2,1},{3,0},{4,7},{5,6},{6,5},{7,4},{8,11},{9,10},{10,... | collective-permute-start | bytes 3080 | tf_op jit(solution)/shard_map/ppermute | solution.py:209
